TPU v7x, 256 devices: a whole 4x4x8 slice. The times are simulated.
256 devices in a mesh: stick: 16 (over y_lo, z), band: 16 (over x, y_hi, core).
Axes of the slice: x: 4, y: 4 (y_hi: 2, y_lo: 2; y = y_hi * 2 + y_lo), z: 8, core: 2. Of those that a mesh axis runs over, the one named last changes fastest.
Arguments:
- sticks: float32 [256, 96, 2048], P('band', None, 'stick'), may hold values from -0.0625 to 0.0625
- stick_columns: int32 [2048], P('stick'), may hold values from -1 to 2303, as said below
Outputs:
- exchange_sticks: float32 [256, 96, 2048], P('band', None, 'stick')
Inputs may be any that keep to these rules, and one draw needn't show every extreme that they name: `stick_columns`: each entry is -1 (an empty slot) or a grid column kx * 48 + ky, and no column appears twice. On each index of the stick axis its 128 slots hold the live sticks first and the empty ones after; one index holds 128 live sticks, another 128 / 4, the others from 32 to 128.
All inputs are finite; a program needn't handle non-finite values.
Results may differ from a plain program's by a relative error of at most 0.0003.
Values sent between devices are 32-bit elements; how exact they have to be, the bound alone decides.
A program may use at most 64 MiB of HBM per device.

v0:
```python
import math

import jax
import jax.numpy as jnp
from jax import lax
from jax.sharding import PartitionSpec as P

G = 48
HALF = 2


HIGHEST = lax.Precision.HIGHEST
BOX_LENGTH = 18.0


def passed_along(shard, axis, by):
    size = lax.axis_size(axis)
    return lax.ppermute(shard, axis, [(i, (i + by) % size) for i in range(size)])


def phase_tables(out_count, in_count, extent):
    row_index = lax.broadcasted_iota(jnp.int32, (out_count, in_count), 0)
    col_index = lax.broadcasted_iota(jnp.int32, (out_count, in_count), 1)
    phase_angle = 2.0 * math.pi / extent * (row_index * col_index % extent).astype(jnp.float32)
    return (jnp.cos(phase_angle), jnp.sin(phase_angle))


def coulomb_kernel(extent):
    half_count = extent // 2 + 1
    frequency = jnp.arange(extent, dtype=jnp.int32)
    folded = jnp.minimum(frequency, extent - frequency)
    squares = folded * folded
    squared_sum = squares[:half_count, None, None] + squares[None, :, None] + squares[None, None, :]
    unit_square = (2.0 * math.pi / BOX_LENGTH) ** 2
    bounded = jnp.maximum(squared_sum, 1).astype(jnp.float32)
    kernel = jnp.where(squared_sum > 0, 4.0 * math.pi / (unit_square * bounded), 0.0)
    return kernel.reshape(half_count, extent * extent)


def matmul(left_side, right_side):
    return jnp.dot(left_side, right_side, precision=HIGHEST, preferred_element_type=jnp.float32)


def contract(values, matrix, pattern, shape_view):
    result = jnp.einsum(
        pattern,
        values.reshape(shape_view),
        matrix,
        precision=HIGHEST,
        preferred_element_type=jnp.float32,
    )
    return result.reshape(result.shape[0], -1)


def complex_step(pair_parts, tables, pattern, shape_view, parity):
    real_part, imag_part = pair_parts
    cos_table, sin_table = tables
    real_cos = contract(real_part, cos_table, pattern, shape_view)
    real_sin = contract(real_part, sin_table, pattern, shape_view)
    imag_cos = contract(imag_part, cos_table, pattern, shape_view)
    imag_sin = contract(imag_part, sin_table, pattern, shape_view)
    return (real_cos - parity * imag_sin, imag_cos + parity * real_sin)


def place_rows(values, slot_rows):
    grid = jnp.zeros((G * G + 1, G), jnp.float32).at[slot_rows].set(values)[: G * G]
    return grid.reshape(G, G * G)


def pick_rows(values, slot_rows):
    padded = jnp.concatenate([values.reshape(G * G, G), jnp.zeros((1, G), jnp.float32)], axis=0)
    return padded[slot_rows]


def potential(density, tables):
    cos_full, sin_full, cos_half, sin_half, back_cos, back_sin, kernel = tables
    half_count = G // 2 + 1
    half_view = (half_count, G, G)
    trig = (cos_full, sin_full)
    pair_parts = (matmul(cos_half, density), -matmul(sin_half, density))
    pair_parts = complex_step(pair_parts, trig, "ayz,yb->azb", half_view, -1.0)
    pair_parts = complex_step(pair_parts, trig, "azb,zc->abc", half_view, -1.0)
    pair_parts = (pair_parts[0] * kernel, pair_parts[1] * kernel)
    pair_parts = complex_step(pair_parts, trig, "abc,by->acy", half_view, 1.0)
    pair_parts = complex_step(pair_parts, trig, "acy,cz->ayz", half_view, 1.0)
    return matmul(back_cos, pair_parts[0]) - matmul(back_sin, pair_parts[1])


def orbital_field(own_rows, slot_rows, tables):
    trig = (tables[0], tables[1])
    full_view = (G, G, G)
    pair_parts = (own_rows[:, :G], own_rows[:, G:])
    pair_parts = (place_rows(pair_parts[0], slot_rows), place_rows(pair_parts[1], slot_rows))
    pair_parts = complex_step(pair_parts, trig, "abc,cz->abz", full_view, 1.0)
    pair_parts = complex_step(pair_parts, trig, "abz,by->ayz", full_view, 1.0)
    return matmul(tables[0], pair_parts[0]) - matmul(tables[1], pair_parts[1])


def exchange_rows(exchange_field, slot_rows, tables):
    trig = (tables[0], tables[1])
    full_view = (G, G, G)
    pair_parts = (matmul(tables[0], exchange_field), -matmul(tables[1], exchange_field))
    pair_parts = complex_step(pair_parts, trig, "ayz,yb->abz", full_view, -1.0)
    pair_parts = complex_step(pair_parts, trig, "abz,zc->abc", full_view, -1.0)
    pair_parts = (pick_rows(pair_parts[0], slot_rows), pick_rows(pair_parts[1], slot_rows))
    return jnp.concatenate([pair_parts[0], pair_parts[1]], axis=1) * G ** (-1.5)


def on_device(sticks, stick_columns):
    half_count = G // 2 + 1
    cos_full, sin_full = phase_tables(G, G, G)
    cos_half, sin_half = phase_tables(half_count, G, G)
    back_cos, back_sin = phase_tables(G, half_count, G)
    freq_index = lax.broadcasted_iota(jnp.int32, (1, half_count), 1)
    weights = jnp.where((freq_index == 0) | (freq_index == G // 2), 1.0, 2.0) / float(G**3)
    tables = (
        cos_full,
        sin_full,
        cos_half,
        sin_half,
        back_cos * weights,
        back_sin * weights,
        coulomb_kernel(G),
    )
    columns = lax.all_gather(stick_columns, "stick", axis=0, tiled=True)
    slot_rows = jnp.where(columns >= 0, columns, G * G)
    own_block = lax.all_to_all(sticks, "stick", split_axis=0, concat_axis=2, tiled=True)[0]
    own_rows = jnp.transpose(own_block)
    orbital = orbital_field(own_rows, slot_rows, tables)

    def pair_term(source):
        return potential(orbital * source, tables) * source

    carried = passed_along(orbital, "band", HALF)
    exchange_field = pair_term(carried)
    for distance in range(2 * HALF):
        carried = passed_along(carried, "band", -1)
        exchange_field = exchange_field + pair_term(carried)
    result = jnp.transpose(exchange_rows(exchange_field, slot_rows, tables))
    return lax.all_to_all(result[None], "stick", split_axis=2, concat_axis=0, tiled=True)


def solution(mesh):
    return jax.shard_map(
        on_device,
        mesh=mesh,
        in_specs=(P("band", None, "stick"), P("stick")),
        out_specs=P("band", None, "stick"),
        check_vma=False,
    )
```

profile of v0, /device:TPU:46, one launch (start us, length us, event | category | flops | bytes accessed | tf_op | source)
XLA Modules:
  0.0 301.5 jit_solution(14420289189548436295)
XLA Ops:
  0.0 9.6 %all-to-all-start = ((f32[16,96,128]{2,1,0:T(8,128)}), f32[16,96,128]{2,1,0:T(8,128)S(1)}, u32[]{:S(2)}, u32[]{:S(2)}) async-start(f32[16,96,128]{2,1,0:T(8,128)} %param.2), calls=%async_computation | async-start | bytes 1572864 | tf_op jit(solution)/shard_map/all_to_all | solution.py:127
  9.6 43.6 %all-gather = s32[16,1,128]{2,1,0:T(1,128)S(1)} all-gather(s32[1,1,128]{2,1,0:T(1,128)S(1)} %bitcast.356), channel_id=1, replica_groups=mesh['stick'=16,'band'=16] {'stick'}, dimensions={0}, use_global_device_ids=true | all-gather | bytes 8704 | tf_op jit(solution)/shard_map/all_gather | solution.py:125
  54.4 5.9 %scatter_custom_fusion = f32[2305,48]{1,0:T(8,128)S(1)} fusion(s32[2048]{0:T(1024)S(1)} %get-tuple-element.8, f32[2048,48]{1,0:T(8,128)S(1)} %copy.295, f32[]{:T(128)} %constant.22.clone.1), kind=kCustom, calls=%fused_computation.127 | custom fusion | bytes 442564 | tf_op jit(solution)/shard_map/scatter | solution.py:66
  60.4 2.2 fusion.216
  62.6 1.3 copy.296
  63.9 6.7 %scatter_custom_fusion.1 = f32[2305,48]{1,0:T(8,128)S(1)} fusion(s32[2048]{0:T(1024)} %copy-done.4, f32[2048,48]{1,0:T(8,128)} %copy.296, f32[]{:T(128)} %constant.22.clone.1), kind=kCustom, calls=%fused_computation.125 | custom fusion | bytes 443072 | tf_op jit(solution)/shard_map/scatter | solution.py:66
  79.3 2.4 fusion.278
  84.6 2.6 collective-permute-start
  87.2 8.3 %collective-permute-done = f32[48,2304]{1,0:T(8,128)S(1)} collective-permute-done((f32[48,2304]{1,0:T(8,128)S(1)}, f32[48,2304]{1,0:T(8,128)S(1)}, u32[]{:S(2)}, u32[]{:S(2)}) %collective-permute-start) | collective-permute-done | bytes 442400 | tf_op jit(solution)/shard_map/ppermute | solution.py:18
  106.7 1.5 fusion.42
  118.0 1.4 fusion
  119.3 3.8 %collective-permute-done.1 = f32[48,2304]{1,0:T(8,128)S(1)} collective-permute-done((f32[48,2304]{1,0:T(8,128)S(1)}, f32[48,2304]{1,0:T(8,128)S(1)}, u32[]{:S(2)}, u32[]{:S(2)}) %collective-permute-start.1) | collective-permute-done | bytes 442400 | tf_op jit(solution)/shard_map/ppermute | solution.py:18
  134.3 1.5 fusion.36
  144.5 4.6 %collective-permute-start.2 = (f32[48,2304]{1,0:T(8,128)S(1)}, f32[48,2304]{1,0:T(8,128)S(1)}, u32[]{:S(2)}, u32[]{:S(2)}) collective-permute-start(f32[48,2304]{1,0:T(8,128)S(1)} %collective-permute-done.1), channel_id=1, source_target_pairs={{0,15},{1,0},{2,1},{3,2},{4,3},{5,4},{6,5},{7,6},{8,7},{9,8},{10,9... | collective-permute-start | bytes 1327112 | tf_op jit(solution)/shard_map/ppermute | solution.py:18
  150.3 4.6 %collective-permute-done.2 = f32[48,2304]{1,0:T(8,128)S(1)} collective-permute-done((f32[48,2304]{1,0:T(8,128)S(1)}, f32[48,2304]{1,0:T(8,128)S(1)}, u32[]{:S(2)}, u32[]{:S(2)}) %collective-permute-start.2) | collective-permute-done | bytes 442400 | tf_op jit(solution)/shard_map/ppermute | solution.py:18
  166.0 1.7 fusion.30
  176.4 4.6 %collective-permute-start.3 = (f32[48,2304]{1,0:T(8,128)S(1)}, f32[48,2304]{1,0:T(8,128)S(1)}, u32[]{:S(2)}, u32[]{:S(2)}) collective-permute-start(f32[48,2304]{1,0:T(8,128)S(1)} %collective-permute-done.2), channel_id=1, source_target_pairs={{0,15},{1,0},{2,1},{3,2},{4,3},{5,4},{6,5},{7,6},{8,7},{9,8},{10,9... | collective-permute-start | bytes 1327112 | tf_op jit(solution)/shard_map/ppermute | solution.py:18
  181.6 1.4 fusion.4
  183.0 3.8 %collective-permute-done.3 = f32[48,2304]{1,0:T(8,128)S(1)} collective-permute-done((f32[48,2304]{1,0:T(8,128)S(1)}, f32[48,2304]{1,0:T(8,128)S(1)}, u32[]{:S(2)}, u32[]{:S(2)}) %collective-permute-start.3) | collective-permute-done | bytes 442400 | tf_op jit(solution)/shard_map/ppermute | solution.py:18
  198.0 1.5 fusion.24
  208.2 4.8 %collective-permute-start.4 = (f32[48,2304]{1,0:T(8,128)S(1)}, f32[48,2304]{1,0:T(8,128)S(1)}, u32[]{:S(2)}, u32[]{:S(2)}) collective-permute-start(f32[48,2304]{1,0:T(8,128)S(1)} %collective-permute-done.3), channel_id=1, source_target_pairs={{0,15},{1,0},{2,1},{3,2},{4,3},{5,4},{6,5},{7,6},{8,7},{9,8},{10,9... | collective-permute-start | bytes 1327112 | tf_op jit(solution)/shard_map/ppermute | solution.py:18
  214.2 4.6 %collective-permute-done.4 = f32[48,2304]{1,0:T(8,128)S(1)} collective-permute-done((f32[48,2304]{1,0:T(8,128)S(1)}, f32[48,2304]{1,0:T(8,128)S(1)}, u32[]{:S(2)}, u32[]{:S(2)}) %collective-permute-start.4) | collective-permute-done | bytes 442400 | tf_op jit(solution)/shard_map/ppermute | solution.py:18
  229.9 1.5 fusion.18
  242.0 1.4 fusion.276
  245.6 1.7 reshape.171
  249.8 1.4 fusion.47
  252.5 1.4 fusion.51
  253.9 1.4 fusion.9
  255.8 1.4 fusion.10
  257.7 5.5 %gather_fusion.1 = f32[2048,48]{1,0:T(8,128)S(1)} fusion(f32[2305,48]{1,0:T(8,128)S(1)} %concatenate.10, s32[2048]{0:T(1024)S(1)} %get-tuple-element.7), kind=kCustom, calls=%fused_computation.1 | custom fusion | bytes 794624 | tf_op jit(solution)/shard_map/gather | solution.py:72
  263.2 5.5 %gather_fusion = f32[2048,48]{1,0:T(8,128)S(1)} fusion(f32[2305,48]{1,0:T(8,128)S(1)} %concatenate.9, s32[2048]{0:T(1024)S(1)} %get-tuple-element.7), kind=kCustom, calls=%fused_computation | custom fusion | bytes 794624 | tf_op jit(solution)/shard_map/gather | solution.py:72
  269.0 31.1 %all_to_all.33 = f32[1,96,2048]{1,0,2:T(1,128)S(1)} all-to-all(f32[1,96,2048]{1,0,2:T(1,128)S(1)} %bitcast.349), channel_id=1, replica_groups=mesh['stick'=16,'band'=16] {'stick'}, dimensions={2} | all-to-all | bytes 1572864 | tf_op jit(solution)/shard_map/all_to_all | solution.py:140
  (159 shorter events, 125.6 us)
Async XLA Ops:
  0.0 9.6 %copy-start.5 = (s32[128]{0:T(128)S(1)}, s32[128]{0:T(128)}, u32[]{:S(2)}) copy-start(s32[128]{0:T(128)} %param.3) | copy-start | bytes 1540
  0.0 53.3 %all-to-all-start = ((f32[16,96,128]{2,1,0:T(8,128)}), f32[16,96,128]{2,1,0:T(8,128)S(1)}, u32[]{:S(2)}, u32[]{:S(2)}) async-start(f32[16,96,128]{2,1,0:T(8,128)} %param.2), calls=%async_computation | async-start | bytes 1572864 | tf_op jit(solution)/shard_map/all_to_all | solution.py:127
  53.3 1.1 copy-start.4
  70.7 1.3 copy-start
  82.9 1.0 copy-start.3
  84.6 11.0 %collective-permute-start = (f32[48,2304]{1,0:T(8,128)S(1)}, f32[48,2304]{1,0:T(8,128)S(1)}, u32[]{:S(2)}, u32[]{:S(2)}) collective-permute-start(f32[48,2304]{1,0:T(8,128)S(1)} %convolution_subtract_fusion.5), channel_id=1, source_target_pairs={{0,2},{1,3},{2,4},{3,5},{4,6},{5,7},{6,8},{7,9},{8,10},{9,11},{10,... | collective-permute-start | bytes 1327112 | tf_op jit(solution)/shard_map/ppermute | solution.py:18
  116.9 6.3 %collective-permute-start.1 = (f32[48,2304]{1,0:T(8,128)S(1)}, f32[48,2304]{1,0:T(8,128)S(1)}, u32[]{:S(2)}, u32[]{:S(2)}) collective-permute-start(f32[48,2304]{1,0:T(8,128)S(1)} %collective-permute-done), channel_id=1, source_target_pairs={{0,15},{1,0},{2,1},{3,2},{4,3},{5,4},{6,5},{7,6},{8,7},{9,8},{10,9... | collective-permute-start | bytes 1327112 | tf_op jit(solution)/shard_map/ppermute | solution.py:18
  144.2 5.5 %copy-start.2 = (f32[48,2304]{1,0:T(8,128)S(1)}, f32[48,2304]{1,0:T(8,128)}, u32[]{:S(2)}) copy-start(f32[48,2304]{1,0:T(8,128)} %fusion) | copy-start | bytes 1327108
  144.5 10.4 %collective-permute-start.2 = (f32[48,2304]{1,0:T(8,128)S(1)}, f32[48,2304]{1,0:T(8,128)S(1)}, u32[]{:S(2)}, u32[]{:S(2)}) collective-permute-start(f32[48,2304]{1,0:T(8,128)S(1)} %collective-permute-done.1), channel_id=1, source_target_pairs={{0,15},{1,0},{2,1},{3,2},{4,3},{5,4},{6,5},{7,6},{8,7},{9,8},{10,9... | collective-permute-start | bytes 1327112 | tf_op jit(solution)/shard_map/ppermute | solution.py:18
  176.4 10.4 %collective-permute-start.3 = (f32[48,2304]{1,0:T(8,128)S(1)}, f32[48,2304]{1,0:T(8,128)S(1)}, u32[]{:S(2)}, u32[]{:S(2)}) collective-permute-start(f32[48,2304]{1,0:T(8,128)S(1)} %collective-permute-done.2), channel_id=1, source_target_pairs={{0,15},{1,0},{2,1},{3,2},{4,3},{5,4},{6,5},{7,6},{8,7},{9,8},{10,9... | collective-permute-start | bytes 1327112 | tf_op jit(solution)/shard_map/ppermute | solution.py:18
  207.8 5.7 %copy-start.1 = (f32[48,2304]{1,0:T(8,128)S(1)}, f32[48,2304]{1,0:T(8,128)}, u32[]{:S(2)}) copy-start(f32[48,2304]{1,0:T(8,128)} %fusion.4) | copy-start | bytes 1327108
  208.2 10.6 %collective-permute-start.4 = (f32[48,2304]{1,0:T(8,128)S(1)}, f32[48,2304]{1,0:T(8,128)S(1)}, u32[]{:S(2)}, u32[]{:S(2)}) collective-permute-start(f32[48,2304]{1,0:T(8,128)S(1)} %collective-permute-done.3), channel_id=1, source_target_pairs={{0,15},{1,0},{2,1},{3,2},{4,3},{5,4},{6,5},{7,6},{8,7},{9,8},{10,9... | collective-permute-start | bytes 1327112 | tf_op jit(solution)/shard_map/ppermute | solution.py:18
where the time goes:
time: 306 us; the launch traced here: 302 us
  matrix products  133 us (43%)
  blocking collectives  74.7 us (24%)
  local copies, waits for them, and re-layouts  40.1 us (13%)
  starting transfers between devices  26.6 us (9%)
  waiting for transfers between devices  25.1 us (8%)
    dot_general x96, matrix products, contract(): jnp.einsum(pattern, values.reshape(shape_view), matrix, precision=HIGHEST...  116 us
    all_gather x1, blocking collectives, on_device(): columns = lax.all_gather(stick_columns, 'stick', axis=0, tiled=True)  43.6 us
    all_to_all x1, blocking collectives, on_device(): lax.all_to_all(result[None], 'stick', split_axis=2, concat_axis=0, tiled=...  31.1 us
    ppermute x5, waiting for transfers between devices, passed_along(): lax.ppermute(shard, axis, [(i, (i + by) % size) for i in range(size)])  25.1 us
    dot_general x24, matrix products, matmul(): jnp.dot(left_side, right_side, precision=HIGHEST, preferred_element_type=...  17.6 us
    ppermute x5, starting transfers between devices, passed_along(): lax.ppermute(shard, axis, [(i, (i + by) % size) for i in range(size)])  17 us
    scatter x2, local copies, waits for them, and re-layouts, place_rows(): jnp.zeros((G * G + 1, G), jnp.float32).at[slot_rows].set(values)[:G * G]  12.5 us
    gather x2, local copies, waits for them, and re-layouts, pick_rows(): return padded[slot_rows]  10.9 us
  transfers between devices with their start and end apart: 6, of which 5 were waited for; matrix products, arithmetic and copies ran while one was open for 2% of the time, Pallas kernels for 0%

commit v1 on v0

v1 whole, which is shorter than its diff:
```python
import functools
import math

import jax
import jax.numpy as jnp
import ml_dtypes
import numpy as np
from jax import lax
from jax.experimental import pallas as pl
from jax.experimental.pallas import tpu as pltpu
from jax.sharding import PartitionSpec as P

G = 48
LANES = G * G
OWNERS = 16
CAP = 128
BOX_LENGTH = 18.0
F32, BF16 = jnp.float32, jnp.bfloat16


def two_parts(table):
    high = table.astype(ml_dtypes.bfloat16)
    low = (table - high.astype(np.float64)).astype(ml_dtypes.bfloat16)
    return high, low


def stacked(table):
    high, low = two_parts(table)
    return np.concatenate([high, high, low], axis=1)


def make_tables():
    index = np.arange(G)
    angle = 2.0 * np.pi / G * (np.outer(index, index) % G)
    cos, sin = np.cos(angle), np.sin(angle)
    plus = (cos + sin) / np.sqrt(G)
    minus = (cos - sin) / np.sqrt(G)
    on_y = np.kron(plus, np.eye(16))
    on_z = np.einsum("aibj,kl->akiblj", plus.reshape(3, 16, 3, 16), np.eye(8)).reshape(384, 384)
    folded = np.minimum(index, G - index).astype(np.float64) ** 2
    total = folded[:, None, None] + folded[None, :, None] + folded[None, None, :]
    kernel = np.where(total > 0, 4.0 * np.pi / ((2.0 * np.pi / BOX_LENGTH) ** 2 * np.maximum(total, 1.0)), 0.0)
    kernel = kernel.reshape(G, 6, 8, 3, 16).transpose(0, 3, 1, 2, 4).reshape(G, LANES)
    z_in = np.block([[cos, -sin], [sin, cos]])
    z_out = np.block([[cos, sin], [-sin, cos]]) * G**-1.5
    return dict(
        x=stacked(plus),
        x_in=stacked(np.concatenate([plus, minus], axis=1) * (0.5 * G)),
        x_out=stacked(np.concatenate([plus, minus], axis=0) * (0.5 * G)),
        y_high=two_parts(on_y)[0],
        y_low=two_parts(on_y)[1],
        z_high=two_parts(on_z)[0],
        z_low=two_parts(on_z)[1],
        kernel=kernel.astype(np.float32),
        z_in=stacked(z_in),
        z_out=stacked(z_out),
    )


TABLES = make_tables()


def dot(left, right):
    return jnp.dot(left, right, preferred_element_type=F32)


def split(value):
    high = value.astype(BF16)
    return high, (value - high.astype(F32)).astype(BF16)


def left_product(table, value):
    high, low = split(value)
    return dot(table, jnp.concatenate([high, low, high], axis=0))


def right_product(value, high_table, low_table):
    high, low = split(value)
    return dot(high, high_table) + dot(low, high_table) + dot(high, low_table)


def y_stage(fields, high, low):
    rows = [f[:, 768 * z : 768 * (z + 1)] for f in fields for z in range(3)]
    out = right_product(jnp.concatenate(rows, axis=0), high, low)
    pieces = [out[G * i : G * (i + 1)] for i in range(len(rows))]
    return [jnp.concatenate(pieces[3 * i : 3 * i + 3], axis=1) for i in range(len(fields))]


def tile(field, z, y):
    start = 128 * (6 * z + y)
    return field[:, start : start + 128]


def z_stage(fields, high, low):
    rows = [jnp.concatenate([tile(f, z, y) for z in range(3)], axis=1) for f in fields for y in range(6)]
    out = right_product(jnp.concatenate(rows, axis=0), high, low)
    pieces = [out[G * i : G * (i + 1)] for i in range(len(rows))]
    return [
        jnp.concatenate([pieces[6 * i + y][:, 128 * z : 128 * (z + 1)] for z in range(3) for y in range(6)], axis=1)
        for i in range(len(fields))
    ]


def reflected(tiles):
    lane = lax.broadcasted_iota(jnp.int32, (G, 128), 1) // 16
    out = []
    for y in range(6):
        source = tiles[5 - y]
        turned = jnp.where(
            lane == 4,
            source,
            jnp.where(
                lane % 4 == 1,
                pltpu.roll(source, 32, 1),
                jnp.where(lane % 4 == 2, pltpu.roll(source, 64, 1), pltpu.roll(source, 96, 1)),
            ),
        )
        out.append(jnp.where(lane == 0, tiles[(6 - y) % 6], turned))
    return out


def slot_places(columns):
    kx = (columns * 43691) >> 21
    ky = columns - kx * G
    row = (ky >> 3) * G + kx
    return jnp.where(columns >= 0, row, -1), ky & 7


def one_hot(row):
    places = lax.broadcasted_iota(jnp.int32, (6 * G, CAP), 0)
    return jnp.where(places == row, 1.0, 0.0).astype(BF16)


def in_kernel(blocks, x_in, y_high, y_low, z_in, orbital):
    groups = lax.broadcasted_iota(jnp.int32, (128, CAP), 0) >> 4

    def place(owner, grid):
        values = blocks[owner, : 2 * G, :]
        columns = blocks[owner, 2 * G : 2 * G + 1, :].astype(jnp.int32)
        row, group = slot_places(columns)
        high, low = split(left_product(z_in[...], values))
        keep = jnp.where(groups == group, 1.0, 0.0).astype(BF16)
        spread = [
            jnp.concatenate([jnp.concatenate([part[16 * t : 16 * t + 16]] * 8, axis=0) * keep for t in range(6)], axis=0)
            for part in (high, low)
        ]
        hot = one_hot(row)
        return grid + lax.dot_general(
            jnp.concatenate([hot, hot], axis=1),
            jnp.concatenate(spread, axis=1),
            (((1,), (1,)), ((), ())),
            preferred_element_type=F32,
        )

    grid = lax.fori_loop(0, OWNERS, place, jnp.zeros((6 * G, 768), F32))

    def tiles(t):
        return [grid[G * y : G * (y + 1), 128 * t : 128 * (t + 1)] for y in range(6)]

    first, second = [], []
    for z in range(3):
        real, imag = tiles(z), tiles(3 + z)
        first += [r - i for r, i in zip(reflected(real), imag)]
        second += [r + i for r, i in zip(real, reflected(imag))]
    pair = y_stage([jnp.concatenate(first, axis=1), jnp.concatenate(second, axis=1)], y_high[...], y_low[...])
    orbital[...] = left_product(x_in[...], jnp.concatenate(pair, axis=0))


def pot_kernel(count, own, *refs):
    sources, (x, y_high, y_low, z_high, z_low, kernel, start, out) = refs[:count], refs[count:]
    fields = [left_product(x[...], own[...] * s[...]) for s in sources]
    fields = y_stage(fields, y_high[...], y_low[...])
    fields = z_stage(fields, z_high[...], z_low[...])
    fields = [f * kernel[...] for f in fields]
    fields = z_stage(fields, z_high[...], z_low[...])
    fields = y_stage(fields, y_high[...], y_low[...])
    total = start[...]
    for f, s in zip(fields, sources):
        total = total + left_product(x[...], f) * s[...]
    out[...] = total


def out_kernel(field, columns, x_out, y_high, y_low, z_out, out, turned):
    pair = left_product(x_out[...], field[...])
    plus, minus = y_stage([pair[:G], pair[G:]], y_high[...], y_low[...])
    real, imag = [], []
    for z in range(3):
        p = [tile(plus, z, y) for y in range(6)]
        m = [tile(minus, z, y) for y in range(6)]
        real.append([a + b for a, b in zip(m, reflected(p))])
        imag.append([a - b for a, b in zip(reflected(m), p)])
    for t, part in enumerate(real + imag):
        column = jnp.concatenate(part + [jnp.zeros((96, 128), F32)], axis=0)
        high, low = split(column.T[:, : 6 * G])
        turned[0, 128 * t : 128 * (t + 1), :] = high
        turned[1, 128 * t : 128 * (t + 1), :] = low
    groups = lax.broadcasted_iota(jnp.int32, (8, CAP), 0)

    def pick(owner, carry):
        row, group = slot_places(columns[owner, :, :].astype(jnp.int32))
        hot = one_hot(row)
        found = dot(turned[0], hot) + dot(turned[1], hot)
        rows = []
        for t in range(6):
            total = jnp.zeros((16, CAP), F32)
            for g in range(8):
                start = 128 * t + 16 * g
                total = total + jnp.where(group == g, found[start : start + 16], 0.0)
            rows.append(total)
        out[owner, :, :] = left_product(z_out[...], jnp.concatenate(rows, axis=0))
        return carry

    lax.fori_loop(0, OWNERS, pick, 0)


def call(kernel, out_shape, args, scratch=(), flops=1e9):
    return pl.pallas_call(
        kernel,
        out_shape=jax.ShapeDtypeStruct(out_shape, F32),
        in_specs=[pl.BlockSpec(memory_space=pltpu.VMEM)] * len(args),
        out_specs=pl.BlockSpec(memory_space=pltpu.VMEM),
        scratch_shapes=list(scratch),
        cost_estimate=pl.CostEstimate(flops=int(flops), bytes_accessed=int(4e6), transcendentals=0),
    )(*args)


def orbital_of(blocks, t):
    return call(in_kernel, (G, LANES), [blocks, t["x_in"], t["y_high"], t["y_low"], t["z_in"]])


def add_pots(own, sources, start, t):
    names = ("x", "y_high", "y_low", "z_high", "z_low", "kernel")
    return call(
        functools.partial(pot_kernel, len(sources)), (G, LANES), [own, *sources, *(t[n] for n in names), start], flops=3e9 * len(sources)
    )


def exchange_of(field, columns, t):
    return call(
        out_kernel,
        (OWNERS, 2 * G, CAP),
        [field, columns, t["x_out"], t["y_high"], t["y_low"], t["z_out"]],
        [pltpu.VMEM((2, 768, 6 * G), BF16)],
    )


def passed_along(shard, axis, by):
    size = lax.axis_size(axis)
    return lax.ppermute(shard, axis, [(i, (i + by) % size) for i in range(size)])


def on_device(sticks, stick_columns):
    t = {name: jnp.asarray(value) for name, value in TABLES.items()}
    labels = jnp.broadcast_to(stick_columns.astype(F32), (OWNERS, 8, CAP))
    sent = jnp.concatenate([sticks, labels], axis=1)
    blocks = lax.all_to_all(sent, "stick", split_axis=0, concat_axis=0, tiled=True)
    orbital = orbital_of(blocks, t)
    near = [passed_along(orbital, "band", by) for by in (1, -1)]
    far = [passed_along(orbital, "band", by) for by in (2, -2)]
    field = add_pots(orbital, [orbital], jnp.zeros((G, LANES), F32), t)
    field = add_pots(orbital, near, field, t)
    field = add_pots(orbital, far, field, t)
    columns = blocks[:, 2 * G : 2 * G + 1, :]
    result = exchange_of(field, columns, t)
    return lax.all_to_all(result, "stick", split_axis=0, concat_axis=0, tiled=True)


def solution(mesh):
    return jax.shard_map(
        on_device,
        mesh=mesh,
        in_specs=(P("band", None, "stick"), P("stick")),
        out_specs=P("band", None, "stick"),
        check_vma=False,
    )
```

time: 306 us -> 136 us (0.44)
  the two profiles are of different devices: /device:TPU:46 before, /device:TPU:5 now
where the time goes in v1:
time: 136 us; the launch traced here: 135 us
  blocking collectives  54 us (40%)
  Pallas kernels  53.3 us (39%)
  waiting for transfers between devices  12.3 us (9%)
  starting transfers between devices  7.68 us (6%)
  local copies, waits for them, and re-layouts  5.73 us (4%)
  other arithmetic  1.85 us (1%)
    pallas_call x5, Pallas kernels, call(): pl.pallas_call(kernel, out_shape=jax.ShapeDtypeStruct(out_shape, F32), in...  53.3 us
    all_to_all x1, blocking collectives, on_device(): lax.all_to_all(sent, 'stick', split_axis=0, concat_axis=0, tiled=True)  30.5 us
    all_to_all x1, blocking collectives, on_device(): lax.all_to_all(result, 'stick', split_axis=0, concat_axis=0, tiled=True)  23.5 us
    ppermute x4, waiting for transfers between devices, passed_along(): lax.ppermute(shard, axis, [(i, (i + by) % size) for i in range(size)])  12.3 us
    ppermute x4, starting transfers between devices, passed_along(): lax.ppermute(shard, axis, [(i, (i + by) % size) for i in range(size)])  7.68 us
    unnamed x9, local copies, waits for them, and re-layouts  3.49 us
  transfers between devices with their start and end apart: 4, of which 2 were waited for; matrix products, arithmetic and copies ran while one was open for 2% of the time, Pallas kernels for 11%

profile of v1, /device:TPU:5, one launch (start us, length us, event | category | flops | bytes accessed | tf_op | source)
XLA Modules:
  0.0 134.9 jit_solution(6031087522944850006)
XLA Ops:
  0.0 0.7 convert_element_type.3
  0.7 1.2 pad_maximum_fusion
  1.9 30.5 %all_to_all.10.blocks = f32[16,104,128]{2,1,0:T(8,128)} all-to-all(f32[16,104,128]{2,1,0:T(8,128)S(1)} %pad_maximum_fusion), channel_id=1, replica_groups=mesh['stick'=16,'band'=16] {'stick'}, dimensions={0} | all-to-all | bytes 1703936 | tf_op jit(solution)/shard_map/all_to_all | solution.py:256
  32.4 14.0 %shard_map.118.own.refs_0_ = f32[48,2304]{1,0:T(8,128)} custom-call(f32[16,104,128]{2,1,0:T(8,128)} %all_to_all.10.blocks, bf16[48,288]{1,0:T(8,128)(2,1)} %constant.23.clone.x_in, bf16[768,768]{1,0:T(8,128)(2,1)} %constant.25.clone.y_high.refs_2_.refs_3_, bf16[768,768]{1,0:T(8,128)(2,1)} %constant.26.clone.y_low.refs_3_.refs_4_, ...), custom_call_target="tpu_custom_call" | custom-call | flops 1000000000 | bytes 4000000 | tf_op jit(solution)/shard_map/pallas_call | solution.py:217
  46.4 2.2 %collective-permute-start.3 = (f32[48,2304]{1,0:T(8,128)}, f32[48,2304]{1,0:T(8,128)S(1)}, u32[]{:S(2)}, u32[]{:S(2)}) collective-permute-start(f32[48,2304]{1,0:T(8,128)} %shard_map.118.own.refs_0_), channel_id=1, source_target_pairs={{0,15},{1,0},{2,1},{3,2},{4,3},{5,4},{6,5},{7,6},{8,7},{9,8},{10,9... | collective-permute-start | bytes 1327112 | tf_op jit(solution)/shard_map/ppermute | solution.py:249
  48.6 2.5 %collective-permute-start.2 = (f32[48,2304]{1,0:T(8,128)}, f32[48,2304]{1,0:T(8,128)S(1)}, u32[]{:S(2)}, u32[]{:S(2)}) collective-permute-start(f32[48,2304]{1,0:T(8,128)} %shard_map.118.own.refs_0_), channel_id=1, source_target_pairs={{0,1},{1,2},{2,3},{3,4},{4,5},{5,6},{6,7},{7,8},{8,9},{9,10},{10,1... | collective-permute-start | bytes 1327112 | tf_op jit(solution)/shard_map/ppermute | solution.py:249
  51.1 2.0 %collective-permute-start.1 = (f32[48,2304]{1,0:T(8,128)}, f32[48,2304]{1,0:T(8,128)S(1)}, u32[]{:S(2)}, u32[]{:S(2)}) collective-permute-start(f32[48,2304]{1,0:T(8,128)} %shard_map.118.own.refs_0_), channel_id=1, source_target_pairs={{0,14},{1,15},{2,0},{3,1},{4,2},{5,3},{6,4},{7,5},{8,6},{9,7},{10,... | collective-permute-start | bytes 1327112 | tf_op jit(solution)/shard_map/ppermute | solution.py:249
  53.1 0.9 collective-permute-start
  54.1 1.4 %slice.4.columns = f32[16,1,128]{2,1,0:T(1,128)} slice(f32[16,104,128]{2,1,0:T(8,128)} %all_to_all.10.blocks), slice={[0:16], [96:97], [0:128]} | slice | bytes 16384 | tf_op jit(solution)/shard_map/slice | solution.py:263
  55.5 0.8 broadcast_in_dim.7.refs_7_
  56.3 6.3 %shard_map.119.refs_8_ = f32[48,2304]{1,0:T(8,128)} custom-call(f32[48,2304]{1,0:T(8,128)} %shard_map.118.own.refs_0_, f32[48,2304]{1,0:T(8,128)} %shard_map.118.own.refs_0_, bf16[48,144]{1,0:T(8,128)(2,1)} %constant.22.clone.refs_1_.refs_2_, bf16[768,768]{1,0:T(8,128)(2,1)} %constant.25.clone.y_high.refs_2_.refs_3_, ...), custom_call_target="tpu_custom_call" | custom-call | flops 3000000000 | bytes 4000000 | tf_op jit(solution)/shard_map/pallas_call | solution.py:217
  62.6 11.8 %collective-permute-done.3.refs_1_ = f32[48,2304]{1,0:T(8,128)S(1)} collective-permute-done((f32[48,2304]{1,0:T(8,128)}, f32[48,2304]{1,0:T(8,128)S(1)}, u32[]{:S(2)}, u32[]{:S(2)}) %collective-permute-start.3) | collective-permute-done | bytes 442400 | tf_op jit(solution)/shard_map/ppermute | solution.py:249
  74.4 0.0 copy-start.2
  74.4 0.5 collective-permute-done.2.refs_0_
  74.9 0.3 copy-done.2
  75.2 0.0 copy-start.3
  75.2 0.8 copy-done.3
  76.0 8.8 %shard_map.120.refs_8_ = f32[48,2304]{1,0:T(8,128)} custom-call(f32[48,2304]{1,0:T(8,128)} %shard_map.118.own.refs_0_, f32[48,2304]{1,0:T(8,128)} %copy-done.3, f32[48,2304]{1,0:T(8,128)} %copy-done.2, bf16[48,144]{1,0:T(8,128)(2,1)} %constant.22.clone.refs_1_.refs_2_, bf16[768,768]{1,0:T(8,128)(2,1)} %constant.25.clone.y_high.refs_2_.refs_3_, ...), custom_call_target="tpu_custom_call" | custom-call | flops 6000000000 | bytes 4000000 | tf_op jit(solution)/shard_map/pallas_call | solution.py:217
  84.8 0.0 collective-permute-done.1.refs_1_
  84.8 0.0 copy-start
  84.8 0.0 collective-permute-done.refs_0_
  84.8 0.8 copy-done
  85.6 0.0 copy-start.1
  85.6 0.8 copy-done.1
  86.4 8.8 %shard_map.121.field = f32[48,2304]{1,0:T(8,128)} custom-call(f32[48,2304]{1,0:T(8,128)} %shard_map.118.own.refs_0_, f32[48,2304]{1,0:T(8,128)} %copy-done.1, f32[48,2304]{1,0:T(8,128)} %copy-done, bf16[48,144]{1,0:T(8,128)(2,1)} %constant.22.clone.refs_1_.refs_2_, bf16[768,768]{1,0:T(8,128)(2,1)} %constant.25.clone.y_high.refs_2_.refs_3_, ...), custom_call_target="tpu_custom_call" | custom-call | flops 6000000000 | bytes 4000000 | tf_op jit(solution)/shard_map/pallas_call | solution.py:217
  95.2 15.3 %shard_map.122 = f32[16,96,128]{2,1,0:T(8,128)} custom-call(f32[48,2304]{1,0:T(8,128)} %shard_map.121.field, f32[16,1,128]{2,1,0:T(1,128)} %slice.4.columns, bf16[96,144]{1,0:T(8,128)(2,1)} %constant.24.clone.x_out, bf16[768,768]{1,0:T(8,128)(2,1)} %constant.25.clone.y_high.refs_2_.refs_3_, bf16[768,768]{1,0:T(8,128)(2,1)} %constant.26.clone.y_low.refs_3_.refs_4_, ...), custom_call_target="tpu_custom_call" | custom-call | flops 1000000000 | bytes 4000000 | tf_op jit(solution)/shard_map/pallas_call | solution.py:217
  110.5 23.5 %all_to_all.11 = f32[16,96,128]{2,1,0:T(8,128)S(1)} all-to-all(f32[16,96,128]{2,1,0:T(8,128)} %shard_map.122), channel_id=1, replica_groups=mesh['stick'=16,'band'=16] {'stick'}, dimensions={0} | all-to-all | bytes 1572864 | tf_op jit(solution)/shard_map/all_to_all | solution.py:265
  134.0 0.9 copy.14
  (1 shorter events, 0.0 us)
Async XLA Ops:
  46.4 28.0 %collective-permute-start.3 = (f32[48,2304]{1,0:T(8,128)}, f32[48,2304]{1,0:T(8,128)S(1)}, u32[]{:S(2)}, u32[]{:S(2)}) collective-permute-start(f32[48,2304]{1,0:T(8,128)} %shard_map.118.own.refs_0_), channel_id=1, source_target_pairs={{0,15},{1,0},{2,1},{3,2},{4,3},{5,4},{6,5},{7,6},{8,7},{9,8},{10,9... | collective-permute-start | bytes 1327112 | tf_op jit(solution)/shard_map/ppermute | solution.py:249
  48.6 26.3 %collective-permute-start.2 = (f32[48,2304]{1,0:T(8,128)}, f32[48,2304]{1,0:T(8,128)S(1)}, u32[]{:S(2)}, u32[]{:S(2)}) collective-permute-start(f32[48,2304]{1,0:T(8,128)} %shard_map.118.own.refs_0_), channel_id=1, source_target_pairs={{0,1},{1,2},{2,3},{3,4},{4,5},{5,6},{6,7},{7,8},{8,9},{9,10},{10,1... | collective-permute-start | bytes 1327112 | tf_op jit(solution)/shard_map/ppermute | solution.py:249
  51.1 33.7 %collective-permute-start.1 = (f32[48,2304]{1,0:T(8,128)}, f32[48,2304]{1,0:T(8,128)S(1)}, u32[]{:S(2)}, u32[]{:S(2)}) collective-permute-start(f32[48,2304]{1,0:T(8,128)} %shard_map.118.own.refs_0_), channel_id=1, source_target_pairs={{0,14},{1,15},{2,0},{3,1},{4,2},{5,3},{6,4},{7,5},{8,6},{9,7},{10,... | collective-permute-start | bytes 1327112 | tf_op jit(solution)/shard_map/ppermute | solution.py:249
  53.1 31.7 %collective-permute-start = (f32[48,2304]{1,0:T(8,128)}, f32[48,2304]{1,0:T(8,128)S(1)}, u32[]{:S(2)}, u32[]{:S(2)}) collective-permute-start(f32[48,2304]{1,0:T(8,128)} %shard_map.118.own.refs_0_), channel_id=1, source_target_pairs={{0,2},{1,3},{2,4},{3,5},{4,6},{5,7},{6,8},{7,9},{8,10},{9,11},{10,... | collective-permute-start | bytes 1327112 | tf_op jit(solution)/shard_map/ppermute | solution.py:249
  74.4 0.8 copy-start.2
  75.2 0.8 copy-start.3
  84.8 0.8 copy-start
  85.6 0.8 copy-start.1

commit v2 on v1

v2 whole, which is shorter than its diff:
```python
import functools
import math

import jax
import jax.numpy as jnp
import ml_dtypes
import numpy as np
from jax import lax
from jax.experimental import pallas as pl
from jax.experimental.pallas import tpu as pltpu
from jax.sharding import PartitionSpec as P

G = 48
ROWS, WIDE = 3 * G, 16 * G
OWNERS = 16
CAP = 128
BOX_LENGTH = 18.0
F32, BF16 = jnp.float32, jnp.bfloat16


def two_parts(table):
    high = table.astype(ml_dtypes.bfloat16)
    low = (table - high.astype(np.float64)).astype(ml_dtypes.bfloat16)
    return high, low


def stacked(table):
    high, low = two_parts(table)
    return np.concatenate([high, high, low], axis=1)


def make_tables():
    index = np.arange(G)
    angle = 2.0 * np.pi / G * (np.outer(index, index) % G)
    cos, sin = np.cos(angle), np.sin(angle)
    plus = (cos + sin) / np.sqrt(G)
    minus = (cos - sin) / np.sqrt(G)
    on_y = np.kron(plus, np.eye(16))
    on_z = np.einsum("aibj,kl->akiblj", plus.reshape(3, 16, 3, 16), np.eye(8)).reshape(384, 384)
    folded = np.minimum(index, G - index).astype(np.float64) ** 2
    total = folded[:, None, None] + folded[None, :, None] + folded[None, None, :]
    kernel = np.where(total > 0, 4.0 * np.pi / ((2.0 * np.pi / BOX_LENGTH) ** 2 * np.maximum(total, 1.0)), 0.0)
    kernel = kernel.reshape(G, 6, 8, 3, 16).transpose(3, 0, 1, 2, 4).reshape(ROWS, WIDE)
    z_in = np.block([[cos, -sin], [sin, cos]])
    z_out = np.block([[cos, sin], [-sin, cos]]) * G**-1.5
    return dict(
        x=stacked(plus),
        x_in=stacked(np.concatenate([plus, minus], axis=1) * (0.5 * G)),
        x_out=stacked(np.concatenate([plus, minus], axis=0) * (0.5 * G)),
        y_high=two_parts(on_y)[0],
        y_low=two_parts(on_y)[1],
        z_high=two_parts(on_z)[0],
        z_low=two_parts(on_z)[1],
        kernel=kernel.astype(np.float32),
        z_in=stacked(z_in),
        z_out=stacked(z_out),
    )


TABLES = make_tables()


def dot(left, right):
    return jnp.dot(left, right, preferred_element_type=F32)


def split(value):
    high = value.astype(BF16)
    return high, (value - high.astype(F32)).astype(BF16)


def left_product(table, value):
    high, low = split(value)
    return dot(table, jnp.concatenate([high, low, high], axis=0))


def right_product(value, high_table, low_table):
    high, low = split(value)
    return dot(high, high_table) + dot(low, high_table) + dot(high, low_table)


MESH = pl.DeviceIdType.MESH
STAGES = tuple(TABLES)


def chip_of(pair):
    place = (pair + 6) % 8
    row = place // 4
    return place + row * (7 - 2 * place), row


def computer_of(pair, core, member):
    x, row = chip_of(pair)
    return row * 8 + member % 8, x * 4 + member // 8 * 2 + core


def role_of(stick, band):
    row, x = stick // 8, band // 4
    place = x + row * (7 - 2 * x)
    return (place + 2) % 8, band % 2, band % 4 // 2 * 8 + stick % 8


def hop_of(step):
    return 2 + (step + 1) // 2 * (1 - 2 * (step % 2))


def member_at(step, stick):
    half, rest = step // 8, step % 8
    return rest % 2 * 8 + (stick % 8 // 2 + hop_of(rest // 2)) % 4 * 2 + half


def owner_at(step, member):
    return step % 2 * 8 + (member % 8 // 2 + 8 - hop_of(step // 4)) % 4 * 2 + step // 2 % 2


def y_stage(field, high, low):
    return right_product(field, high, low)


def z_stage(field, high, low):
    rows = [
        jnp.concatenate([field[G * z : G * (z + 1), 128 * y : 128 * (y + 1)] for z in range(3)], axis=1) for y in range(6)
    ]
    out = right_product(jnp.concatenate(rows, axis=0), high, low)
    return jnp.concatenate(
        [
            jnp.concatenate([out[G * y : G * (y + 1), 128 * z : 128 * (z + 1)] for y in range(6)], axis=1)
            for z in range(3)
        ],
        axis=0,
    )


def x_stage(field, table):
    return jnp.concatenate([left_product(table, field[G * z : G * (z + 1)]) for z in range(3)], axis=0)


def reflected(tiles):
    lane = lax.broadcasted_iota(jnp.int32, (G, 128), 1) // 16
    out = []
    for y in range(6):
        source = tiles[5 - y]
        turned = jnp.where(
            lane == 4,
            source,
            jnp.where(
                lane % 4 == 1,
                pltpu.roll(source, 32, 1),
                jnp.where(lane % 4 == 2, pltpu.roll(source, 64, 1), pltpu.roll(source, 96, 1)),
            ),
        )
        out.append(jnp.where(lane == 0, tiles[(6 - y) % 6], turned))
    return out


def slot_places(columns):
    kx = (columns * 43691) >> 21
    ky = columns - kx * G
    row = (ky >> 3) * G + kx
    return jnp.where(columns >= 0, row, -1), ky & 7


def one_hot(row):
    places = lax.broadcasted_iota(jnp.int32, (6 * G, CAP), 0)
    return jnp.where(places == row, 1.0, 0.0).astype(BF16)


def exchange_kernel(sticks, labels, *refs):
    count = len(STAGES)
    stored, out, held = refs[:count], refs[count], refs[count + 1 : 2 * count + 1]
    t = dict(zip(STAGES, held))
    (blocks, columns, grid, fields, total, turned, found, table_sem, in_send, in_recv, label_send, label_recv,
     field_send, field_recv, out_send, out_recv) = refs[2 * count + 1 :]
    stick, band = lax.axis_index("stick"), lax.axis_index("band")
    pair, core, member = role_of(stick, band)
    group = 2 * pair + core

    loads = [pltpu.make_async_copy(a, b, table_sem.at[i]) for i, (a, b) in enumerate(zip(stored, held))]
    for load in loads:
        load.start()

    def own_computer(member):
        return computer_of(band // 2, band % 2, member)

    def mine(device):
        return jnp.logical_and(device[0] == stick, device[1] == band)

    upper, lower = (pair + 1) % 8, (pair + 7) % 8
    to_upper, to_lower = computer_of(upper, 0, member), computer_of(lower, 1, member)
    partner = computer_of(pair, 1 - core, member)
    beyond = core * upper + (1 - core) * lower
    from_first, from_second = computer_of(beyond, 0, member), computer_of(beyond, 1, member)

    barrier = pltpu.get_barrier_semaphore()

    def signal(device):
        pl.semaphore_signal(barrier, 1, device_id=device, device_id_type=MESH)

    def greet(i, carry):
        for device in ((i, group), own_computer(i)):

            @pl.when(jnp.logical_not(mine(device)))
            def _():
                signal(device)

        return carry

    lax.fori_loop(0, OWNERS, greet, 0)
    for device in (from_first, from_second, partner):
        signal(device)

    pl.semaphore_wait(barrier, 2 * OWNERS + 3 - 2 * jnp.where(group == band, 1, 0))

    def stick_copies(i):
        device = own_computer(i)
        pairs = (
            (sticks.at[i], blocks.at[stick], in_send.at[i], in_recv.at[stick]),
            (labels, columns.at[stick], label_send.at[i], label_recv.at[stick]),
        )
        local = [pltpu.make_async_copy(a, b, r) for a, b, s, r in pairs]
        remote = [
            pltpu.make_async_remote_copy(a, b, s, r, device_id=device, device_id_type=MESH) for a, b, s, r in pairs
        ]
        return mine(device), local, remote

    def send(step, carry):
        here, local, remote = stick_copies(member_at(step, stick))

        @pl.when(here)
        def _():
            for copy in local:
                copy.start()

        @pl.when(jnp.logical_not(here))
        def _():
            for copy in remote:
                copy.start()

        return carry

    lax.fori_loop(0, OWNERS, send, 0)

    grid[...] = jnp.zeros_like(grid)
    for load in loads:
        load.wait()
    spans = lax.broadcasted_iota(jnp.int32, (128, CAP), 0) >> 4

    def place(step, carry):
        owner = owner_at(step, member)
        pltpu.make_async_copy(blocks.at[owner], blocks.at[owner], in_recv.at[owner]).wait()
        pltpu.make_async_copy(columns.at[owner], columns.at[owner], label_recv.at[owner]).wait()
        row, span = slot_places(columns[owner])
        high, low = split(left_product(t["z_in"][...], blocks[owner]))
        keep = jnp.where(spans == span, 1.0, 0.0).astype(BF16)
        spread = [
            jnp.concatenate([jnp.concatenate([part[16 * i : 16 * i + 16]] * 8, axis=0) * keep for i in range(6)], axis=0)
            for part in (high, low)
        ]
        hot = one_hot(row)
        grid[...] += lax.dot_general(
            jnp.concatenate([hot, hot], axis=1),
            jnp.concatenate(spread, axis=1),
            (((1,), (1,)), ((), ())),
            preferred_element_type=F32,
        )
        return carry

    lax.fori_loop(0, OWNERS, place, 0)

    def tiles(i):
        return [grid[G * y : G * (y + 1), 128 * i : 128 * (i + 1)] for y in range(6)]

    first, second = [], []
    for z in range(3):
        real, imag = tiles(z), tiles(3 + z)
        first.append(jnp.concatenate([a - b for a, b in zip(reflected(real), imag)], axis=1))
        second.append(jnp.concatenate([a + b for a, b in zip(real, reflected(imag))], axis=1))
    both = y_stage(jnp.concatenate(first + second, axis=0), t["y_high"][...], t["y_low"][...])
    for z in range(3):
        rows = jnp.concatenate([both[G * z : G * (z + 1)], both[ROWS + G * z : ROWS + G * (z + 1)]], axis=0)
        fields[0, G * z : G * (z + 1), :] = left_product(t["x_in"][...], rows)

    def field_copy(source, slot, index, device):
        return pltpu.make_async_remote_copy(
            fields.at[source], fields.at[slot], field_send.at[index], field_recv.at[slot], device_id=device, device_id_type=MESH
        )

    outward = [field_copy(0, 2 + core, 0, to_upper), field_copy(0, 2 + core, 1, to_lower), field_copy(0, 1, 2, partner)]
    for copy in outward:
        copy.start()
    onward = field_copy(3 - core, 4, 3, partner)

    def arrive(slot):
        pltpu.make_async_copy(fields.at[slot], fields.at[slot], field_recv.at[slot]).wait()

    total[...] = jnp.zeros_like(total)

    def pot(slot, carry):
        @pl.when(slot == 1)
        def _():
            arrive(1)

        @pl.when(slot == 2)
        def _():
            arrive(2)
            arrive(3)
            onward.start()

        @pl.when(slot == 4)
        def _():
            arrive(4)

        value = x_stage(fields[0] * fields[slot], t["x"][...])
        value = y_stage(value, t["y_high"][...], t["y_low"][...])
        value = z_stage(value, t["z_high"][...], t["z_low"][...])
        value = value * t["kernel"][...]
        value = z_stage(value, t["z_high"][...], t["z_low"][...])
        value = y_stage(value, t["y_high"][...], t["y_low"][...])
        total[...] += x_stage(value, t["x"][...]) * fields[slot]
        return carry

    lax.fori_loop(0, 5, pot, 0)
    for copy in outward:
        copy.wait_send()
    onward.wait_send()

    split_x = [left_product(t["x_out"][...], total[G * z : G * (z + 1), :]) for z in range(3)]
    both = y_stage(
        jnp.concatenate([v[:G] for v in split_x] + [v[G:] for v in split_x], axis=0), t["y_high"][...], t["y_low"][...]
    )

    def out_tiles(i):
        return [both[G * i : G * (i + 1), 128 * y : 128 * (y + 1)] for y in range(6)]

    real, imag = [], []
    for z in range(3):
        plus, minus = out_tiles(z), out_tiles(3 + z)
        real.append([a + b for a, b in zip(minus, reflected(plus))])
        imag.append([a - b for a, b in zip(reflected(minus), plus)])
    for i, part in enumerate(real + imag):
        column = jnp.concatenate(part + [jnp.zeros((96, 128), F32)], axis=0)
        high, low = split(column.T[:, : 6 * G])
        turned[0, 128 * i : 128 * (i + 1), :] = high
        turned[1, 128 * i : 128 * (i + 1), :] = low

    def result_copies(owner):
        device = (owner, group)
        local = pltpu.make_async_copy(found.at[owner], out.at[member], out_recv.at[member])
        remote = pltpu.make_async_remote_copy(
            found.at[owner], out.at[member], out_send.at[owner], out_recv.at[member], device_id=device, device_id_type=MESH
        )
        return mine(device), local, remote

    def pick(step, carry):
        owner = owner_at(step, member)
        row, span = slot_places(columns[owner])
        hot = one_hot(row)
        picked = dot(turned[0], hot) + dot(turned[1], hot)
        rows = []
        for i in range(6):
            value = jnp.zeros((16, CAP), F32)
            for g in range(8):
                start = 128 * i + 16 * g
                value = value + jnp.where(span == g, picked[start : start + 16], 0.0)
            rows.append(value)
        found[owner] = left_product(t["z_out"][...], jnp.concatenate(rows, axis=0))
        here, local, remote = result_copies(owner)

        @pl.when(here)
        def _():
            local.start()

        @pl.when(jnp.logical_not(here))
        def _():
            remote.start()

        return carry

    lax.fori_loop(0, OWNERS, pick, 0)

    def finish(i, carry):
        here, _, remote = stick_copies(i)

        @pl.when(jnp.logical_not(here))
        def _():
            for copy in remote:
                copy.wait_send()

        here, _, remote = result_copies(i)

        @pl.when(jnp.logical_not(here))
        def _():
            remote.wait_send()

        pltpu.make_async_copy(out.at[i], out.at[i], out_recv.at[i]).wait()
        return carry

    lax.fori_loop(0, OWNERS, finish, 0)


def on_device(sticks, stick_columns):
    tables = [jnp.asarray(TABLES[name]) for name in STAGES]
    anywhere = pl.BlockSpec(memory_space=pl.ANY)
    dma = pltpu.SemaphoreType.DMA
    return pl.pallas_call(
        exchange_kernel,
        out_shape=jax.ShapeDtypeStruct((OWNERS, 2 * G, CAP), F32),
        in_specs=[anywhere, pl.BlockSpec(memory_space=pltpu.VMEM)] + [anywhere] * len(tables),
        out_specs=anywhere,
        scratch_shapes=[pltpu.VMEM(t.shape, t.dtype) for t in tables]
        + [
            pltpu.VMEM((OWNERS, 2 * G, CAP), F32),
            pltpu.VMEM((OWNERS, 1, CAP), jnp.int32),
            pltpu.VMEM((6 * G, WIDE), F32),
            pltpu.VMEM((5, ROWS, WIDE), F32),
            pltpu.VMEM((ROWS, WIDE), F32),
            pltpu.VMEM((2, WIDE, 6 * G), BF16),
            pltpu.VMEM((OWNERS, 2 * G, CAP), F32),
            dma((len(tables),)),
        ]
        + [dma((OWNERS,))] * 4
        + [dma((4,)), dma((5,)), dma((OWNERS,)), dma((OWNERS,))],
        compiler_params=pltpu.CompilerParams(collective_id=0, has_side_effects=True, vmem_limit_bytes=56 << 20),
    )(sticks, stick_columns.reshape(1, CAP), *tables)


def solution(mesh):
    return jax.shard_map(
        on_device,
        mesh=mesh,
        in_specs=(P("band", None, "stick"), P("stick")),
        out_specs=P("band", None, "stick"),
        check_vma=False,
    )
```

time: 136 us -> 91 us (0.67)
  the two profiles are of different devices: /device:TPU:5 before, /device:TPU:63 now
where the time goes in v2:
time: 91 us; the launch traced here: 90.9 us
  Pallas kernels  88.8 us (98%)
  local copies, waits for them, and re-layouts  2.07 us (2%)
    pallas_call x1, Pallas kernels, on_device(): pl.pallas_call(exchange_kernel, out_shape=jax.ShapeDtypeStruct((OWNERS, 2...  88.8 us
    unnamed x1, local copies, waits for them, and re-layouts  2.07 us

profile of v2, /device:TPU:63, one launch (start us, length us, event | category | flops | bytes accessed | tf_op | source)
XLA Modules:
  0.0 90.9 jit_solution(62449748490079496)
XLA Ops:
  0.0 88.8 %shard_map.118 = f32[16,96,128]{2,1,0:T(8,128)} custom-call(f32[16,96,128]{2,1,0:T(8,128)} %sticks.1, s32[1,128]{1,0:T(1,128)} %bitcast.1, bf16[48,144]{1,0:T(8,128)(2,1)} %constant.20.clone.refs_0_, bf16[48,288]{1,0:T(8,128)(2,1)} %constant.21.clone.refs_1_, bf16[96,144]{1,0:T(8,128)(2,1)} %constant.22.clone.refs_2_, ...), custom_call_target="tpu_custom_call" | custom-call | tf_op jit(solution)/shard_map/pallas_call | solution.py:405
  88.8 2.1 %copy.14 = f32[16,96,128]{2,1,0:T(8,128)} copy(f32[16,96,128]{2,1,0:T(8,128)} %shard_map.118) | data formatting | bytes 1572864

commit v3 on v2

v3 whole, which is shorter than its diff:
```python
import functools
import math

import jax
import jax.numpy as jnp
import ml_dtypes
import numpy as np
from jax import lax
from jax.experimental import pallas as pl
from jax.experimental.pallas import tpu as pltpu
from jax.sharding import PartitionSpec as P

G = 48
ROWS, WIDE = 3 * G, 16 * G
OWNERS = 16
CAP = 128
BOX_LENGTH = 18.0
F32, BF16 = jnp.float32, jnp.bfloat16


def two_parts(table):
    high = table.astype(ml_dtypes.bfloat16)
    low = (table - high.astype(np.float64)).astype(ml_dtypes.bfloat16)
    return high, low


def stacked(table):
    high, low = two_parts(table)
    return np.concatenate([high, high, low], axis=1)


def make_tables():
    index = np.arange(G)
    angle = 2.0 * np.pi / G * (np.outer(index, index) % G)
    cos, sin = np.cos(angle), np.sin(angle)
    plus = (cos + sin) / np.sqrt(G)
    minus = (cos - sin) / np.sqrt(G)
    on_y = np.kron(plus, np.eye(16))
    on_z = np.einsum("aibj,kl->akiblj", plus.reshape(3, 16, 3, 16), np.eye(8)).reshape(384, 384)
    folded = np.minimum(index, G - index).astype(np.float64) ** 2
    total = folded[:, None, None] + folded[None, :, None] + folded[None, None, :]
    kernel = np.where(total > 0, 4.0 * np.pi / ((2.0 * np.pi / BOX_LENGTH) ** 2 * np.maximum(total, 1.0)), 0.0)
    kernel = kernel.reshape(G, 6, 8, 3, 16).transpose(3, 0, 1, 2, 4).reshape(ROWS, WIDE)
    z_in = np.block([[cos, -sin], [sin, cos]]).reshape(2, 3, 16, 2 * G).transpose(1, 0, 2, 3).reshape(2 * G, 2 * G)
    z_out = np.block([[cos, sin], [-sin, cos]])
    return dict(
        x=stacked(plus),
        x_in=stacked(np.concatenate([plus, minus], axis=1) * (0.5 * G)),
        x_out=stacked(np.concatenate([plus, minus], axis=0) * (0.5 * G)),
        y_high=two_parts(on_y)[0],
        y_low=two_parts(on_y)[1],
        z_high=two_parts(on_z)[0],
        z_low=two_parts(on_z)[1],
        kernel=kernel.astype(np.float32),
        z_in=stacked(z_in),
        z_out=stacked(z_out),
    )


TABLES = make_tables()


def dot(left, right):
    return jnp.dot(left, right, preferred_element_type=F32)


def split(value):
    high = value.astype(BF16)
    return high, (value - high.astype(F32)).astype(BF16)


def left_product(table, value):
    high, low = split(value)
    return dot(table, jnp.concatenate([high, low, high], axis=0))


def right_product(value, high_table, low_table):
    high, low = split(value)
    return dot(high, high_table) + dot(low, high_table) + dot(high, low_table)


MESH = pl.DeviceIdType.MESH
STAGES = tuple(TABLES)


def chip_of(pair):
    place = (pair + 6) % 8
    row = place // 4
    return place + row * (7 - 2 * place), row


def computer_of(pair, core, member):
    x, row = chip_of(pair)
    return row * 8 + member % 8, x * 4 + member // 8 * 2 + core


def role_of(stick, band):
    row, x = stick // 8, band // 4
    place = x + row * (7 - 2 * x)
    return (place + 2) % 8, band % 2, band % 4 // 2 * 8 + stick % 8


def y_stage(field, high, low):
    return right_product(field, high, low)


def z_stage(field, high, low):
    rows = [
        jnp.concatenate([field[G * z : G * (z + 1), 128 * y : 128 * (y + 1)] for z in range(3)], axis=1) for y in range(6)
    ]
    out = right_product(jnp.concatenate(rows, axis=0), high, low)
    return jnp.concatenate(
        [
            jnp.concatenate([out[G * y : G * (y + 1), 128 * z : 128 * (z + 1)] for y in range(6)], axis=1)
            for z in range(3)
        ],
        axis=0,
    )


def x_stage(field, table):
    return jnp.concatenate([left_product(table, field[G * z : G * (z + 1)]) for z in range(3)], axis=0)


def reflected(tiles):
    lane = lax.broadcasted_iota(jnp.int32, (G, 128), 1) // 16
    out = []
    for y in range(6):
        source = tiles[5 - y]
        turned = jnp.where(
            lane == 4,
            source,
            jnp.where(
                lane % 4 == 1,
                pltpu.roll(source, 32, 1),
                jnp.where(lane % 4 == 2, pltpu.roll(source, 64, 1), pltpu.roll(source, 96, 1)),
            ),
        )
        out.append(jnp.where(lane == 0, tiles[(6 - y) % 6], turned))
    return out


def slot_places(columns):
    kx = (columns * 43691) >> 21
    ky = columns - kx * G
    row = (ky >> 3) * G + kx
    return jnp.where(columns >= 0, row, -1), ky & 7


def one_hot(row):
    places = lax.broadcasted_iota(jnp.int32, (6 * G, row.shape[1]), 0)
    return jnp.where(places == row, 1.0, 0.0).astype(BF16)


def exchange_kernel(sticks, labels, *refs):
    count = len(STAGES)
    stored, out, held = refs[:count], refs[count], refs[count + 1 : 2 * count + 1]
    t = dict(zip(STAGES, held))
    (sent, blocks, columns, grid, fields, total, turned, found, table_sem, in_send, in_recv, label_send, label_recv,
     field_send, field_recv, out_send, out_recv) = refs[2 * count + 1 :]
    stick, band = lax.axis_index("stick"), lax.axis_index("band")
    pair, core, member = role_of(stick, band)
    group = 2 * pair + core

    loads = [pltpu.make_async_copy(a, b, table_sem.at[i]) for i, (a, b) in enumerate(zip(stored, held))]
    for load in loads:
        load.start()

    def own_computer(member):
        return computer_of(band // 2, band % 2, member)

    def mine(device):
        return jnp.logical_and(device[0] == stick, device[1] == band)

    upper, lower = (pair + 1) % 8, (pair + 7) % 8
    to_upper, to_lower = computer_of(upper, 0, member), computer_of(lower, 1, member)
    partner = computer_of(pair, 1 - core, member)
    beyond = core * upper + (1 - core) * lower
    from_first, from_second = computer_of(beyond, 0, member), computer_of(beyond, 1, member)

    barrier = pltpu.get_barrier_semaphore()

    def signal(device):
        pl.semaphore_signal(barrier, 1, device_id=device, device_id_type=MESH)

    def greet(i, carry):
        for device in ((i, group), own_computer(i)):

            @pl.when(jnp.logical_not(mine(device)))
            def _():
                signal(device)

        return carry

    lax.fori_loop(0, OWNERS, greet, 0)
    for device in (from_first, from_second, partner):
        signal(device)

    for load in loads:
        load.wait()

    def to_planes(i, carry):
        sent[i] = left_product(t["z_in"][...], sticks[i])
        return carry

    lax.fori_loop(0, OWNERS, to_planes, 0)
    pl.semaphore_wait(barrier, 2 * OWNERS + 3 - 2 * jnp.where(group == band, 1, 0))

    def either(device, source, target, out_sem, in_sem, start):
        @pl.when(mine(device))
        def _():
            if start:
                pltpu.make_async_copy(source, target, in_sem).start()

        @pl.when(jnp.logical_not(mine(device)))
        def _():
            copy = pltpu.make_async_remote_copy(
                source, target, out_sem, in_sem, device_id=device, device_id_type=MESH
            )
            if start:
                copy.start()
            else:
                copy.wait_send()

    def label_copy(i, start):
        either(own_computer(i), labels, columns.at[stick], label_send.at[i], label_recv.at[stick], start)

    def plane_copy(z, i, start):
        source, target = sent.at[i, pl.ds(pl.multiple_of(32 * z, 32), 32)], blocks.at[z, stick]
        either(own_computer(i), source, target, in_send.at[z, i], in_recv.at[z, stick], start)

    def send_labels(step, carry):
        label_copy((stick + step) % OWNERS, True)
        return carry

    def send_planes(index, carry):
        plane_copy(index // OWNERS, (stick + index) % OWNERS, True)
        return carry

    lax.fori_loop(0, OWNERS, send_labels, 0)
    lax.fori_loop(0, 3 * OWNERS, send_planes, 0)

    spans = lax.broadcasted_iota(jnp.int32, (128, CAP), 0) >> 4

    def arrive(ref, sem):
        pltpu.make_async_copy(ref, ref, sem).wait()

    def field_copy(source, slot, z, index, device):
        return pltpu.make_async_remote_copy(
            fields.at[source, z],
            fields.at[slot, z],
            field_send.at[index, z],
            field_recv.at[slot, z],
            device_id=device,
            device_id_type=MESH,
        )

    def outward(z):
        return [
            field_copy(0, 2 + core, z, 0, to_upper),
            field_copy(0, 2 + core, z, 1, to_lower),
            field_copy(0, 1, z, 2, partner),
        ]

    def onward(z):
        return field_copy(3 - core, 4, z, 3, partner)

    def plane(z, carry):
        grid[...] = jnp.zeros_like(grid)

        def place(step, carry):
            owner = (member + OWNERS - step) % OWNERS

            @pl.when(z == 0)
            def _():
                arrive(columns.at[owner], label_recv.at[owner])

            arrive(blocks.at[z, owner], in_recv.at[z, owner])
            row, span = slot_places(columns[owner])
            high, low = split(blocks[z, owner])
            keep = jnp.where(spans == span, 1.0, 0.0).astype(BF16)
            spread = [
                jnp.concatenate([jnp.concatenate([part[16 * i : 16 * i + 16]] * 8, axis=0) * keep for i in range(2)], axis=0)
                for part in (high, low)
            ]
            hot = one_hot(row)
            grid[...] += lax.dot_general(
                jnp.concatenate([hot, hot], axis=1),
                jnp.concatenate(spread, axis=1),
                (((1,), (1,)), ((), ())),
                preferred_element_type=F32,
            )
            return carry

        lax.fori_loop(0, OWNERS, place, 0)
        real = [grid[G * y : G * (y + 1), :128] for y in range(6)]
        imag = [grid[G * y : G * (y + 1), 128:] for y in range(6)]
        first = jnp.concatenate([a - b for a, b in zip(reflected(real), imag)], axis=1)
        second = jnp.concatenate([a + b for a, b in zip(real, reflected(imag))], axis=1)
        both = y_stage(jnp.concatenate([first, second], axis=0), t["y_high"][...], t["y_low"][...])
        fields[0, z] = left_product(t["x_in"][...], both)
        for copy in outward(z):
            copy.start()

        @pl.when(z > 0)
        def _():
            arrive(fields.at[3 - core, z - 1], field_recv.at[3 - core, z - 1])
            onward(z - 1).start()

        return carry

    lax.fori_loop(0, 3, plane, 0)
    total[...] = jnp.zeros_like(total)

    def arrive_field(slot):
        for z in range(3):
            arrive(fields.at[slot, z], field_recv.at[slot, z])

    def pot(slot, carry):
        @pl.when(slot == 1)
        def _():
            arrive_field(1)

        @pl.when(slot == 2)
        def _():
            arrive(fields.at[3 - core, 2], field_recv.at[3 - core, 2])
            onward(2).start()
            arrive_field(2 + core)

        @pl.when(slot == 4)
        def _():
            arrive_field(4)

        source = fields[slot].reshape(ROWS, WIDE)
        value = x_stage(fields[0].reshape(ROWS, WIDE) * source, t["x"][...])
        value = y_stage(value, t["y_high"][...], t["y_low"][...])
        value = z_stage(value, t["z_high"][...], t["z_low"][...])
        value = value * t["kernel"][...]
        value = z_stage(value, t["z_high"][...], t["z_low"][...])
        value = y_stage(value, t["y_high"][...], t["y_low"][...])
        total[...] += x_stage(value, t["x"][...]) * source
        return carry

    lax.fori_loop(0, 5, pot, 0)
    for z in range(3):
        for copy in outward(z):
            copy.wait_send()
        onward(z).wait_send()

    split_x = [left_product(t["x_out"][...], total[G * z : G * (z + 1), :]) for z in range(3)]
    both = y_stage(
        jnp.concatenate([v[:G] for v in split_x] + [v[G:] for v in split_x], axis=0), t["y_high"][...], t["y_low"][...]
    )

    def out_tiles(i):
        return [both[G * i : G * (i + 1), 128 * y : 128 * (y + 1)] for y in range(6)]

    real, imag = [], []
    for z in range(3):
        plus, minus = out_tiles(z), out_tiles(3 + z)
        real.append([a + b for a, b in zip(minus, reflected(plus))])
        imag.append([a - b for a, b in zip(reflected(minus), plus)])
    for i, part in enumerate(real + imag):
        column = jnp.concatenate(part + [jnp.zeros((96, 128), F32)], axis=0)
        high, low = split(column.T[:, : 6 * G])
        turned[128 * i : 128 * (i + 1), : 6 * G] = high
        turned[128 * i : 128 * (i + 1), 6 * G :] = low

    def result_copy(owner, start):
        either((owner, group), found.at[owner], out.at[member], out_send.at[owner], out_recv.at[member], start)

    def pick(step, carry):
        owners = [(member + OWNERS - 2 * step - i) % OWNERS for i in range(2)]
        row, span = slot_places(jnp.concatenate([columns[owner] for owner in owners], axis=1))
        hot = one_hot(row)
        picked = dot(turned[...], jnp.concatenate([hot, hot], axis=0))
        rows = []
        for i in range(6):
            value = jnp.zeros((16, 2 * CAP), F32)
            for g in range(8):
                start = 128 * i + 16 * g
                value = value + jnp.where(span == g, picked[start : start + 16], 0.0)
            rows.append(value)
        result = left_product(t["z_out"][...], jnp.concatenate(rows, axis=0))
        for i, owner in enumerate(owners):
            found[owner] = result[:, CAP * i : CAP * (i + 1)]
            result_copy(owner, True)
        return carry

    lax.fori_loop(0, OWNERS // 2, pick, 0)

    def finish(i, carry):
        label_copy(i, False)
        for z in range(3):
            plane_copy(z, i, False)
        result_copy(i, False)
        arrive(out.at[i], out_recv.at[i])
        return carry

    lax.fori_loop(0, OWNERS, finish, 0)


def on_device(sticks, stick_columns):
    tables = [jnp.asarray(TABLES[name]) for name in STAGES]
    anywhere = pl.BlockSpec(memory_space=pl.ANY)
    dma = pltpu.SemaphoreType.DMA
    result = pl.pallas_call(
        exchange_kernel,
        out_shape=jax.ShapeDtypeStruct((OWNERS, 2 * G, CAP), F32),
        in_specs=[pl.BlockSpec(memory_space=pltpu.VMEM)] * 2 + [anywhere] * len(tables),
        out_specs=anywhere,
        scratch_shapes=[pltpu.VMEM(t.shape, t.dtype) for t in tables]
        + [
            pltpu.VMEM((OWNERS, 2 * G, CAP), F32),
            pltpu.VMEM((3, OWNERS, 32, CAP), F32),
            pltpu.VMEM((OWNERS, 1, CAP), jnp.int32),
            pltpu.VMEM((6 * G, 256), F32),
            pltpu.VMEM((5, 3, G, WIDE), F32),
            pltpu.VMEM((ROWS, WIDE), F32),
            pltpu.VMEM((WIDE, 12 * G), BF16),
            pltpu.VMEM((OWNERS, 2 * G, CAP), F32),
            dma((len(tables),)),
            dma((3, OWNERS)),
            dma((3, OWNERS)),
            dma((OWNERS,)),
            dma((OWNERS,)),
            dma((4, 3)),
            dma((5, 3)),
            dma((OWNERS,)),
            dma((OWNERS,)),
        ],
        compiler_params=pltpu.CompilerParams(collective_id=0, has_side_effects=True, vmem_limit_bytes=56 << 20),
    )(sticks, stick_columns.reshape(1, CAP), *tables)
    return result * np.float32(G**-1.5)


def solution(mesh):
    return jax.shard_map(
        on_device,
        mesh=mesh,
        in_specs=(P("band", None, "stick"), P("stick")),
        out_specs=P("band", None, "stick"),
        check_vma=False,
    )
```

time: 91 us -> 83.3 us (0.915)
  the two profiles are of different devices: /device:TPU:63 before, /device:TPU:5 now
where the time goes in v3:
time: 83.3 us; the launch traced here: 83.1 us
  Pallas kernels  81 us (97%)
  other arithmetic  2.08 us (2%)
    pallas_call x1, Pallas kernels, on_device(): pl.pallas_call(exchange_kernel, out_shape=jax.ShapeDtypeStruct((OWNERS, 2...  81 us
    mul x1, other arithmetic, on_device(): return result * np.float32(G ** (-1.5))  2.08 us

profile of v3, /device:TPU:5, one launch (start us, length us, event | category | flops | bytes accessed | tf_op | source)
XLA Modules:
  0.0 83.1 jit_solution(3399361040403907546)
XLA Ops:
  0.0 81.0 %shard_map.118 = f32[16,96,128]{2,1,0:T(8,128)} custom-call(f32[16,96,128]{2,1,0:T(8,128)} %sticks.1, s32[1,128]{1,0:T(1,128)} %bitcast.1, bf16[48,144]{1,0:T(8,128)(2,1)} %constant.22.clone.refs_0_, bf16[48,288]{1,0:T(8,128)(2,1)} %constant.23.clone.refs_1_, bf16[96,144]{1,0:T(8,128)(2,1)} %constant.24.clone.refs_2_, ...), custom_call_target="tpu_custom_call" | custom-call | tf_op jit(solution)/shard_map/pallas_call | solution.py:407
  81.0 2.1 %broadcast_multiply_fusion = f32[16,96,128]{2,1,0:T(8,128)} fusion(f32[16,96,128]{2,1,0:T(8,128)} %shard_map.118), kind=kLoop, calls=%fused_computation | loop fusion | flops 196608 | bytes 1572864 | tf_op jit(solution)/shard_map/mul | solution.py:434

commit v4 on v3

--- a/solution.py
+++ b/solution.py
@@ -76,7 +76,9 @@
 
 def right_product(value, high_table, low_table):
     high, low = split(value)
-    return dot(high, high_table) + dot(low, high_table) + dot(high, low_table)
+    rows = value.shape[0]
+    both = dot(jnp.concatenate([high, low], axis=0), high_table)
+    return both[:rows] + both[rows:] + dot(high, low_table)
 
 
 MESH = pl.DeviceIdType.MESH
@@ -105,13 +107,17 @@
 
 
 def z_stage(field, high, low):
+    starts = range(0, field.shape[0], ROWS)
     rows = [
-        jnp.concatenate([field[G * z : G * (z + 1), 128 * y : 128 * (y + 1)] for z in range(3)], axis=1) for y in range(6)
+        jnp.concatenate([field[a + G * z : a + G * (z + 1), 128 * y : 128 * (y + 1)] for z in range(3)], axis=1)
+        for a in starts
+        for y in range(6)
     ]
     out = right_product(jnp.concatenate(rows, axis=0), high, low)
     return jnp.concatenate(
         [
-            jnp.concatenate([out[G * y : G * (y + 1), 128 * z : 128 * (z + 1)] for y in range(6)], axis=1)
+            jnp.concatenate([out[2 * a + G * y : 2 * a + G * (y + 1), 128 * z : 128 * (z + 1)] for y in range(6)], axis=1)
+            for a in starts
             for z in range(3)
         ],
         axis=0,
@@ -119,7 +125,7 @@
 
 
 def x_stage(field, table):
-    return jnp.concatenate([left_product(table, field[G * z : G * (z + 1)]) for z in range(3)], axis=0)
+    return jnp.concatenate([left_product(table, field[G * z : G * (z + 1)]) for z in range(field.shape[0] // G)], axis=0)
 
 
 def reflected(tiles):
@@ -156,21 +162,17 @@
     count = len(STAGES)
     stored, out, held = refs[:count], refs[count], refs[count + 1 : 2 * count + 1]
     t = dict(zip(STAGES, held))
-    (sent, blocks, columns, grid, fields, total, turned, found, table_sem, in_send, in_recv, label_send, label_recv,
+    (given, sent, blocks, columns, grid, fields, total, turned, found, table_sem, in_send, in_recv, label_send, label_recv,
      field_send, field_recv, out_send, out_recv) = refs[2 * count + 1 :]
     stick, band = lax.axis_index("stick"), lax.axis_index("band")
     pair, core, member = role_of(stick, band)
     group = 2 * pair + core
 
-    loads = [pltpu.make_async_copy(a, b, table_sem.at[i]) for i, (a, b) in enumerate(zip(stored, held))]
-    for load in loads:
-        load.start()
-
-    def own_computer(member):
-        return computer_of(band // 2, band % 2, member)
-
-    def mine(device):
-        return jnp.logical_and(device[0] == stick, device[1] == band)
+    home = group == band
+    own_row, own_column = computer_of(band // 2, band % 2, 0)
+
+    def own_computer(i):
+        return own_row + i % 8, own_column + i // 8 * 2
 
     upper, lower = (pair + 1) % 8, (pair + 7) % 8
     to_upper, to_lower = computer_of(upper, 0, member), computer_of(lower, 1, member)
@@ -184,11 +186,13 @@
         pl.semaphore_signal(barrier, 1, device_id=device, device_id_type=MESH)
 
     def greet(i, carry):
-        for device in ((i, group), own_computer(i)):
-
-            @pl.when(jnp.logical_not(mine(device)))
-            def _():
-                signal(device)
+        @pl.when(jnp.logical_not(jnp.logical_and(home, i == stick)))
+        def _():
+            signal((i, group))
+
+        @pl.when(jnp.logical_not(jnp.logical_and(home, i == member)))
+        def _():
+            signal(own_computer(i))
 
         return carry
 
@@ -196,23 +200,36 @@
     for device in (from_first, from_second, partner):
         signal(device)
 
-    for load in loads:
-        load.wait()
+    own_load = pltpu.make_async_copy(sticks, given, table_sem.at[count])
+    own_load.start()
+    loads = [pltpu.make_async_copy(a, b, table_sem.at[i]) for i, (a, b) in enumerate(zip(stored, held))]
+    first_load = STAGES.index("z_in")
+    loads[first_load].start()
+    for i, load in enumerate(loads):
+        if i != first_load:
+            load.start()
+    loads[first_load].wait()
+    own_load.wait()
 
     def to_planes(i, carry):
-        sent[i] = left_product(t["z_in"][...], sticks[i])
-        return carry
-
-    lax.fori_loop(0, OWNERS, to_planes, 0)
-    pl.semaphore_wait(barrier, 2 * OWNERS + 3 - 2 * jnp.where(group == band, 1, 0))
-
-    def either(device, source, target, out_sem, in_sem, start):
-        @pl.when(mine(device))
-        def _():
-            if start:
+        pair = jnp.concatenate([given[2 * i], given[2 * i + 1]], axis=1)
+        pair = left_product(t["z_in"][...], pair)
+        sent[2 * i] = pair[:, :CAP]
+        sent[2 * i + 1] = pair[:, CAP:]
+        return carry
+
+    lax.fori_loop(0, OWNERS // 2, to_planes, 0)
+    pl.semaphore_wait(barrier, 2 * OWNERS + 3 - 2 * jnp.where(home, 1, 0))
+
+    def either(same, device, source, target, out_sem, in_sem, start):
+        here = jnp.logical_and(home, same)
+        if start:
+
+            @pl.when(here)
+            def _():
                 pltpu.make_async_copy(source, target, in_sem).start()
 
-        @pl.when(jnp.logical_not(mine(device)))
+        @pl.when(jnp.logical_not(here))
         def _():
             copy = pltpu.make_async_remote_copy(
                 source, target, out_sem, in_sem, device_id=device, device_id_type=MESH
@@ -223,11 +240,11 @@
                 copy.wait_send()
 
     def label_copy(i, start):
-        either(own_computer(i), labels, columns.at[stick], label_send.at[i], label_recv.at[stick], start)
+        either(i == member, own_computer(i), labels, columns.at[stick], label_send.at[i], label_recv.at[stick], start)
 
     def plane_copy(z, i, start):
         source, target = sent.at[i, pl.ds(pl.multiple_of(32 * z, 32), 32)], blocks.at[z, stick]
-        either(own_computer(i), source, target, in_send.at[z, i], in_recv.at[z, stick], start)
+        either(i == member, own_computer(i), source, target, in_send.at[z, i], in_recv.at[z, stick], start)
 
     def send_labels(step, carry):
         label_copy((stick + step) % OWNERS, True)
@@ -269,30 +286,44 @@
         grid[...] = jnp.zeros_like(grid)
 
         def place(step, carry):
-            owner = (member + OWNERS - step) % OWNERS
+            owners = [(member + OWNERS - 4 * step - i) % OWNERS for i in range(4)]
 
             @pl.when(z == 0)
             def _():
-                arrive(columns.at[owner], label_recv.at[owner])
-
-            arrive(blocks.at[z, owner], in_recv.at[z, owner])
-            row, span = slot_places(columns[owner])
-            high, low = split(blocks[z, owner])
-            keep = jnp.where(spans == span, 1.0, 0.0).astype(BF16)
-            spread = [
-                jnp.concatenate([jnp.concatenate([part[16 * i : 16 * i + 16]] * 8, axis=0) * keep for i in range(2)], axis=0)
-                for part in (high, low)
-            ]
-            hot = one_hot(row)
+                for owner in owners:
+                    arrive(columns.at[owner], label_recv.at[owner])
+
+            hots, spreads = [], []
+            for owner in owners:
+                arrive(blocks.at[z, owner], in_recv.at[z, owner])
+            for owner in owners:
+                row, span = slot_places(columns[owner])
+                keep = jnp.where(spans == span, 1.0, 0.0).astype(BF16)
+                for part in split(blocks[z, owner]):
+                    parts = [jnp.concatenate([part[16 * i : 16 * i + 16]] * 8, axis=0) * keep for i in range(2)]
+                    spreads.append(jnp.concatenate(parts, axis=0))
+                hots += [one_hot(row)] * 2
             grid[...] += lax.dot_general(
-                jnp.concatenate([hot, hot], axis=1),
-                jnp.concatenate(spread, axis=1),
+                jnp.concatenate(hots, axis=1),
+                jnp.concatenate(spreads, axis=1),
                 (((1,), (1,)), ((), ())),
                 preferred_element_type=F32,
             )
             return carry
 
-        lax.fori_loop(0, OWNERS, place, 0)
+        lax.fori_loop(0, OWNERS // 4, place, 0)
+
+        @pl.when(z == 0)
+        def _():
+            for i, load in enumerate(loads):
+                if i != first_load:
+                    load.wait()
+
+        @pl.when(z > 0)
+        def _():
+            arrive(fields.at[3 - core, z - 1], field_recv.at[3 - core, z - 1])
+            onward(z - 1).start()
+
         real = [grid[G * y : G * (y + 1), :128] for y in range(6)]
         imag = [grid[G * y : G * (y + 1), 128:] for y in range(6)]
         first = jnp.concatenate([a - b for a, b in zip(reflected(real), imag)], axis=1)
@@ -302,46 +333,33 @@
         for copy in outward(z):
             copy.start()
 
-        @pl.when(z > 0)
-        def _():
-            arrive(fields.at[3 - core, z - 1], field_recv.at[3 - core, z - 1])
-            onward(z - 1).start()
-
         return carry
 
     lax.fori_loop(0, 3, plane, 0)
-    total[...] = jnp.zeros_like(total)
-
     def arrive_field(slot):
         for z in range(3):
             arrive(fields.at[slot, z], field_recv.at[slot, z])
 
-    def pot(slot, carry):
-        @pl.when(slot == 1)
-        def _():
-            arrive_field(1)
-
-        @pl.when(slot == 2)
-        def _():
-            arrive(fields.at[3 - core, 2], field_recv.at[3 - core, 2])
-            onward(2).start()
-            arrive_field(2 + core)
-
-        @pl.when(slot == 4)
-        def _():
-            arrive_field(4)
-
-        source = fields[slot].reshape(ROWS, WIDE)
-        value = x_stage(fields[0].reshape(ROWS, WIDE) * source, t["x"][...])
+    def pots(slots):
+        sources = [fields[slot].reshape(ROWS, WIDE) for slot in slots]
+        own = fields[0].reshape(ROWS, WIDE)
+        value = jnp.concatenate([own * source for source in sources], axis=0)
+        value = x_stage(value, t["x"][...])
         value = y_stage(value, t["y_high"][...], t["y_low"][...])
         value = z_stage(value, t["z_high"][...], t["z_low"][...])
-        value = value * t["kernel"][...]
+        value = value * jnp.concatenate([t["kernel"][...]] * len(slots), axis=0)
         value = z_stage(value, t["z_high"][...], t["z_low"][...])
         value = y_stage(value, t["y_high"][...], t["y_low"][...])
-        total[...] += x_stage(value, t["x"][...]) * source
-        return carry
-
-    lax.fori_loop(0, 5, pot, 0)
+        value = x_stage(value, t["x"][...])
+        return sum(value[ROWS * i : ROWS * (i + 1)] * source for i, source in enumerate(sources))
+
+    arrive_field(1)
+    total[...] = pots((0, 1))
+    arrive(fields.at[3 - core, 2], field_recv.at[3 - core, 2])
+    onward(2).start()
+    arrive_field(2 + core)
+    arrive_field(4)
+    total[...] += pots((2, 3, 4))
     for z in range(3):
         for copy in outward(z):
             copy.wait_send()
@@ -361,13 +379,12 @@
         real.append([a + b for a, b in zip(minus, reflected(plus))])
         imag.append([a - b for a, b in zip(reflected(minus), plus)])
     for i, part in enumerate(real + imag):
-        column = jnp.concatenate(part + [jnp.zeros((96, 128), F32)], axis=0)
-        high, low = split(column.T[:, : 6 * G])
+        high, low = split(jnp.concatenate(part, axis=0).T)
         turned[128 * i : 128 * (i + 1), : 6 * G] = high
         turned[128 * i : 128 * (i + 1), 6 * G :] = low
 
     def result_copy(owner, start):
-        either((owner, group), found.at[owner], out.at[member], out_send.at[owner], out_recv.at[member], start)
+        either(owner == stick, (owner, group), found.at[owner], out.at[member], out_send.at[owner], out_recv.at[member], start)
 
     def pick(step, carry):
         owners = [(member + OWNERS - 2 * step - i) % OWNERS for i in range(2)]
@@ -407,10 +424,11 @@
     result = pl.pallas_call(
         exchange_kernel,
         out_shape=jax.ShapeDtypeStruct((OWNERS, 2 * G, CAP), F32),
-        in_specs=[pl.BlockSpec(memory_space=pltpu.VMEM)] * 2 + [anywhere] * len(tables),
+        in_specs=[anywhere] * (2 + len(tables)),
         out_specs=anywhere,
         scratch_shapes=[pltpu.VMEM(t.shape, t.dtype) for t in tables]
         + [
+            pltpu.VMEM((OWNERS, 2 * G, CAP), F32),
             pltpu.VMEM((OWNERS, 2 * G, CAP), F32),
             pltpu.VMEM((3, OWNERS, 32, CAP), F32),
             pltpu.VMEM((OWNERS, 1, CAP), jnp.int32),
@@ -419,7 +437,7 @@
             pltpu.VMEM((ROWS, WIDE), F32),
             pltpu.VMEM((WIDE, 12 * G), BF16),
             pltpu.VMEM((OWNERS, 2 * G, CAP), F32),
-            dma((len(tables),)),
+            dma((len(tables) + 1,)),
             dma((3, OWNERS)),
             dma((3, OWNERS)),
             dma((OWNERS,)),

time: 83.3 us -> 82.7 us (level)
  Pallas kernels: 81 us -> 79.8 us
    pallas_call x1, Pallas kernels: 81 us -> 79.8 us  [on_device(): pl.pallas_call(exchange_kernel, out_shape=jax.ShapeDtypeStruct((OWNERS, 2...]
where the time goes in v4:
time: 82.7 us; the launch traced here: 81.9 us
  Pallas kernels  79.8 us (96%)
  other arithmetic  2.08 us (3%)
    pallas_call x1, Pallas kernels, on_device(): pl.pallas_call(exchange_kernel, out_shape=jax.ShapeDtypeStruct((OWNERS, 2...  79.8 us
    mul x1, other arithmetic, on_device(): return result * np.float32(G ** (-1.5))  2.08 us

profile of v4, /device:TPU:5, one launch (start us, length us, event | category | flops | bytes accessed | tf_op | source)
XLA Modules:
  0.0 81.9 jit_solution(1577983102048026357)
XLA Ops:
  0.0 79.8 %shard_map.118 = f32[16,96,128]{2,1,0:T(8,128)} custom-call(f32[16,96,128]{2,1,0:T(8,128)} %sticks.1, s32[1,128]{1,0:T(1,128)} %bitcast.1, bf16[48,144]{1,0:T(8,128)(2,1)} %constant.22.clone.refs_0_, bf16[48,288]{1,0:T(8,128)(2,1)} %constant.23.clone.refs_1_, bf16[96,144]{1,0:T(8,128)(2,1)} %constant.24.clone.refs_2_, ...), custom_call_target="tpu_custom_call" | custom-call | tf_op jit(solution)/shard_map/pallas_call | solution.py:424
  79.8 2.1 %broadcast_multiply_fusion = f32[16,96,128]{2,1,0:T(8,128)} fusion(f32[16,96,128]{2,1,0:T(8,128)} %shard_map.118), kind=kLoop, calls=%fused_computation | loop fusion | flops 196608 | bytes 1572864 | tf_op jit(solution)/shard_map/mul | solution.py:452

commit v5 on v4

--- a/solution.py
+++ b/solution.py
@@ -42,15 +42,14 @@
     kernel = np.where(total > 0, 4.0 * np.pi / ((2.0 * np.pi / BOX_LENGTH) ** 2 * np.maximum(total, 1.0)), 0.0)
     kernel = kernel.reshape(G, 6, 8, 3, 16).transpose(3, 0, 1, 2, 4).reshape(ROWS, WIDE)
     z_in = np.block([[cos, -sin], [sin, cos]]).reshape(2, 3, 16, 2 * G).transpose(1, 0, 2, 3).reshape(2 * G, 2 * G)
-    z_out = np.block([[cos, sin], [-sin, cos]])
+    z_out = np.block([[cos, sin], [-sin, cos]]).reshape(2 * G, 2, 3, 16).transpose(0, 2, 1, 3).reshape(2 * G, 2 * G)
     return dict(
         x=stacked(plus),
         x_in=stacked(np.concatenate([plus, minus], axis=1) * (0.5 * G)),
         x_out=stacked(np.concatenate([plus, minus], axis=0) * (0.5 * G)),
         y_high=two_parts(on_y)[0],
         y_low=two_parts(on_y)[1],
-        z_high=two_parts(on_z)[0],
-        z_low=two_parts(on_z)[1],
+        z=stacked(on_z.T).T.copy(),
         kernel=kernel.astype(np.float32),
         z_in=stacked(z_in),
         z_out=stacked(z_out),
@@ -106,14 +105,15 @@
     return right_product(field, high, low)
 
 
-def z_stage(field, high, low):
+def z_stage(field, table):
     starts = range(0, field.shape[0], ROWS)
     rows = [
         jnp.concatenate([field[a + G * z : a + G * (z + 1), 128 * y : 128 * (y + 1)] for z in range(3)], axis=1)
         for a in starts
         for y in range(6)
     ]
-    out = right_product(jnp.concatenate(rows, axis=0), high, low)
+    high, low = split(jnp.concatenate(rows, axis=0))
+    out = dot(jnp.concatenate([high, low, high], axis=1), table)
     return jnp.concatenate(
         [
             jnp.concatenate([out[2 * a + G * y : 2 * a + G * (y + 1), 128 * z : 128 * (z + 1)] for y in range(6)], axis=1)
@@ -162,8 +162,8 @@
     count = len(STAGES)
     stored, out, held = refs[:count], refs[count], refs[count + 1 : 2 * count + 1]
     t = dict(zip(STAGES, held))
-    (given, sent, blocks, columns, grid, fields, total, turned, found, table_sem, in_send, in_recv, label_send, label_recv,
-     field_send, field_recv, out_send, out_recv) = refs[2 * count + 1 :]
+    (given, sent, blocks, columns, grid, fields, work, total, turned, found, back, ready, table_sem, in_send, in_recv,
+     label_send, label_recv, field_send, field_recv, out_send, out_recv, out_store) = refs[2 * count + 1 :]
     stick, band = lax.axis_index("stick"), lax.axis_index("band")
     pair, core, member = role_of(stick, band)
     group = 2 * pair + core
@@ -281,6 +281,10 @@
 
     def onward(z):
         return field_copy(3 - core, 4, z, 3, partner)
+
+    def pass_on(z):
+        arrive(fields.at[3 - core, z], field_recv.at[3 - core, z])
+        onward(z).start()
 
     def plane(z, carry):
         grid[...] = jnp.zeros_like(grid)
@@ -319,10 +323,9 @@
                 if i != first_load:
                     load.wait()
 
-        @pl.when(z > 0)
-        def _():
-            arrive(fields.at[3 - core, z - 1], field_recv.at[3 - core, z - 1])
-            onward(z - 1).start()
+        @pl.when(z == 2)
+        def _():
+            pass_on(0)
 
         real = [grid[G * y : G * (y + 1), :128] for y in range(6)]
         imag = [grid[G * y : G * (y + 1), 128:] for y in range(6)]
@@ -336,82 +339,101 @@
         return carry
 
     lax.fori_loop(0, 3, plane, 0)
-    def arrive_field(slot):
-        for z in range(3):
-            arrive(fields.at[slot, z], field_recv.at[slot, z])
-
-    def pots(slots):
-        sources = [fields[slot].reshape(ROWS, WIDE) for slot in slots]
-        own = fields[0].reshape(ROWS, WIDE)
-        value = jnp.concatenate([own * source for source in sources], axis=0)
-        value = x_stage(value, t["x"][...])
-        value = y_stage(value, t["y_high"][...], t["y_low"][...])
-        value = z_stage(value, t["z_high"][...], t["z_low"][...])
-        value = value * jnp.concatenate([t["kernel"][...]] * len(slots), axis=0)
-        value = z_stage(value, t["z_high"][...], t["z_low"][...])
-        value = y_stage(value, t["y_high"][...], t["y_low"][...])
-        value = x_stage(value, t["x"][...])
-        return sum(value[ROWS * i : ROWS * (i + 1)] * source for i, source in enumerate(sources))
-
-    arrive_field(1)
-    total[...] = pots((0, 1))
-    arrive(fields.at[3 - core, 2], field_recv.at[3 - core, 2])
-    onward(2).start()
-    arrive_field(2 + core)
-    arrive_field(4)
-    total[...] += pots((2, 3, 4))
+    pass_on(1)
+
+    own = fields[0].reshape(ROWS, WIDE)
+    value = x_stage(own * own, t["x"][...])
+    value = y_stage(value, t["y_high"][...], t["y_low"][...])
+    value = z_stage(value, t["z"][...]) * t["kernel"][...]
+    value = y_stage(z_stage(value, t["z"][...]), t["y_high"][...], t["y_low"][...])
+    total[...] = (x_stage(value, t["x"][...]) * own).reshape(3, G, WIDE)
+
+    def forward(z, carry):
+        @pl.when(z == 1)
+        def _():
+            pass_on(2)
+
+        arrive(fields.at[1, z], field_recv.at[1, z])
+        arrive(fields.at[2 + core, z], field_recv.at[2 + core, z])
+        arrive(fields.at[4, z], field_recv.at[4, z])
+        value = jnp.concatenate([fields[0, z] * fields[slot, z] for slot in range(1, 5)], axis=0)
+        value = y_stage(x_stage(value, t["x"][...]), t["y_high"][...], t["y_low"][...])
+        for i in range(4):
+            work[i, z] = value[G * i : G * (i + 1)]
+        return carry
+
+    lax.fori_loop(0, 3, forward, 0)
+    value = z_stage(work[...].reshape(4 * ROWS, WIDE), t["z"][...])
+    value = value * jnp.concatenate([t["kernel"][...]] * 4, axis=0)
+    work[...] = z_stage(value, t["z"][...]).reshape(4, 3, G, WIDE)
+
+    def result_copy(z, owner, start):
+        device = (owner, group)
+        source, target = found.at[z, owner], back.at[member, z]
+        either(owner == stick, device, source, target, out_send.at[z, owner], out_recv.at[member, z], start)
+
+    def backward(z, carry):
+        value = jnp.concatenate([work[i, z] for i in range(4)], axis=0)
+        value = x_stage(y_stage(value, t["y_high"][...], t["y_low"][...]), t["x"][...])
+        field = total[z]
+        for i in range(4):
+            field = field + value[G * i : G * (i + 1)] * fields[i + 1, z]
+        both = y_stage(left_product(t["x_out"][...], field), t["y_high"][...], t["y_low"][...])
+        plus, minus = [[both[a : a + G, 128 * y : 128 * (y + 1)] for y in range(6)] for a in (0, G)]
+        real = [a + b for a, b in zip(minus, reflected(plus))]
+        imag = [a - b for a, b in zip(reflected(minus), plus)]
+        for i, part in enumerate((real, imag)):
+            high, low = split(jnp.concatenate(part, axis=0).T)
+            turned[128 * i : 128 * (i + 1), : 6 * G] = high
+            turned[128 * i : 128 * (i + 1), 6 * G :] = low
+
+        def pick(step, carry):
+            owners = [(member + OWNERS - 2 * step - i) % OWNERS for i in range(2)]
+            row, span = slot_places(jnp.concatenate([columns[owner] for owner in owners], axis=1))
+            hot = one_hot(row)
+            picked = dot(turned[...], jnp.concatenate([hot, hot], axis=0))
+            rows = []
+            for i in range(2):
+                value = jnp.zeros((16, 2 * CAP), F32)
+                for g in range(8):
+                    start = 128 * i + 16 * g
+                    value = value + jnp.where(span == g, picked[start : start + 16], 0.0)
+                rows.append(value)
+            result = jnp.concatenate(rows, axis=0)
+            for i, owner in enumerate(owners):
+                found[z, owner] = result[:, CAP * i : CAP * (i + 1)]
+                result_copy(z, owner, True)
+            return carry
+
+        lax.fori_loop(0, OWNERS // 2, pick, 0)
+        return carry
+
+    lax.fori_loop(0, 3, backward, 0)
+
+    def from_planes(step, carry):
+        bands = [(stick + 2 * step + i) % OWNERS for i in range(2)]
+        for band_index in bands:
+            for z in range(3):
+                arrive(back.at[band_index, z], out_recv.at[band_index, z])
+        pair = jnp.concatenate([back[band_index].reshape(2 * G, CAP) for band_index in bands], axis=1)
+        pair = left_product(t["z_out"][...], pair)
+        for i, band_index in enumerate(bands):
+            ready[band_index] = pair[:, CAP * i : CAP * (i + 1)]
+            pltpu.make_async_copy(ready.at[band_index], out.at[band_index], out_store.at[band_index]).start()
+        return carry
+
+    lax.fori_loop(0, OWNERS // 2, from_planes, 0)
     for z in range(3):
         for copy in outward(z):
             copy.wait_send()
         onward(z).wait_send()
 
-    split_x = [left_product(t["x_out"][...], total[G * z : G * (z + 1), :]) for z in range(3)]
-    both = y_stage(
-        jnp.concatenate([v[:G] for v in split_x] + [v[G:] for v in split_x], axis=0), t["y_high"][...], t["y_low"][...]
-    )
-
-    def out_tiles(i):
-        return [both[G * i : G * (i + 1), 128 * y : 128 * (y + 1)] for y in range(6)]
-
-    real, imag = [], []
-    for z in range(3):
-        plus, minus = out_tiles(z), out_tiles(3 + z)
-        real.append([a + b for a, b in zip(minus, reflected(plus))])
-        imag.append([a - b for a, b in zip(reflected(minus), plus)])
-    for i, part in enumerate(real + imag):
-        high, low = split(jnp.concatenate(part, axis=0).T)
-        turned[128 * i : 128 * (i + 1), : 6 * G] = high
-        turned[128 * i : 128 * (i + 1), 6 * G :] = low
-
-    def result_copy(owner, start):
-        either(owner == stick, (owner, group), found.at[owner], out.at[member], out_send.at[owner], out_recv.at[member], start)
-
-    def pick(step, carry):
-        owners = [(member + OWNERS - 2 * step - i) % OWNERS for i in range(2)]
-        row, span = slot_places(jnp.concatenate([columns[owner] for owner in owners], axis=1))
-        hot = one_hot(row)
-        picked = dot(turned[...], jnp.concatenate([hot, hot], axis=0))
-        rows = []
-        for i in range(6):
-            value = jnp.zeros((16, 2 * CAP), F32)
-            for g in range(8):
-                start = 128 * i + 16 * g
-                value = value + jnp.where(span == g, picked[start : start + 16], 0.0)
-            rows.append(value)
-        result = left_product(t["z_out"][...], jnp.concatenate(rows, axis=0))
-        for i, owner in enumerate(owners):
-            found[owner] = result[:, CAP * i : CAP * (i + 1)]
-            result_copy(owner, True)
-        return carry
-
-    lax.fori_loop(0, OWNERS // 2, pick, 0)
-
     def finish(i, carry):
         label_copy(i, False)
         for z in range(3):
             plane_copy(z, i, False)
-        result_copy(i, False)
-        arrive(out.at[i], out_recv.at[i])
+            result_copy(z, i, False)
+        pltpu.make_async_copy(ready.at[i], out.at[i], out_store.at[i]).wait()
         return carry
 
     lax.fori_loop(0, OWNERS, finish, 0)
@@ -419,12 +441,12 @@
 
 def on_device(sticks, stick_columns):
     tables = [jnp.asarray(TABLES[name]) for name in STAGES]
-    anywhere = pl.BlockSpec(memory_space=pl.ANY)
+    anywhere, hbm = pl.BlockSpec(memory_space=pl.ANY), pl.BlockSpec(memory_space=pltpu.HBM)
     dma = pltpu.SemaphoreType.DMA
     result = pl.pallas_call(
         exchange_kernel,
         out_shape=jax.ShapeDtypeStruct((OWNERS, 2 * G, CAP), F32),
-        in_specs=[anywhere] * (2 + len(tables)),
+        in_specs=[hbm] * (2 + len(tables)),
         out_specs=anywhere,
         scratch_shapes=[pltpu.VMEM(t.shape, t.dtype) for t in tables]
         + [
@@ -434,8 +456,11 @@
             pltpu.VMEM((OWNERS, 1, CAP), jnp.int32),
             pltpu.VMEM((6 * G, 256), F32),
             pltpu.VMEM((5, 3, G, WIDE), F32),
-            pltpu.VMEM((ROWS, WIDE), F32),
-            pltpu.VMEM((WIDE, 12 * G), BF16),
+            pltpu.VMEM((4, 3, G, WIDE), F32),
+            pltpu.VMEM((3, G, WIDE), F32),
+            pltpu.VMEM((256, 12 * G), BF16),
+            pltpu.VMEM((3, OWNERS, 32, CAP), F32),
+            pltpu.VMEM((OWNERS, 3, 32, CAP), F32),
             pltpu.VMEM((OWNERS, 2 * G, CAP), F32),
             dma((len(tables) + 1,)),
             dma((3, OWNERS)),
@@ -444,7 +469,8 @@
             dma((OWNERS,)),
             dma((4, 3)),
             dma((5, 3)),
-            dma((OWNERS,)),
+            dma((3, OWNERS)),
+            dma((OWNERS, 3)),
             dma((OWNERS,)),
         ],
         compiler_params=pltpu.CompilerParams(collective_id=0, has_side_effects=True, vmem_limit_bytes=56 << 20),

time: 82.7 us -> 74.3 us (0.90)
  Pallas kernels: 79.8 us -> 71.5 us
    pallas_call x1, Pallas kernels: 79.8 us -> 71.5 us  [on_device(): pl.pallas_call(exchange_kernel, out_shape=jax.ShapeDtypeStruct((OWNERS, 2...]
where the time goes in v5:
time: 74.3 us; the launch traced here: 73.6 us
  Pallas kernels  71.5 us (96%)
  other arithmetic  2.08 us (3%)
    pallas_call x1, Pallas kernels, on_device(): pl.pallas_call(exchange_kernel, out_shape=jax.ShapeDtypeStruct((OWNERS, 2...  71.5 us
    mul x1, other arithmetic, on_device(): return result * np.float32(G ** (-1.5))  2.08 us

profile of v5, /device:TPU:5, one launch (start us, length us, event | category | flops | bytes accessed | tf_op | source)
XLA Modules:
  0.0 73.6 jit_solution(12594850431080945130)
XLA Ops:
  0.0 71.5 %shard_map.109 = f32[16,96,128]{2,1,0:T(8,128)} custom-call(f32[16,96,128]{2,1,0:T(8,128)} %sticks.1, s32[1,128]{1,0:T(1,128)} %bitcast.1, bf16[48,144]{1,0:T(8,128)(2,1)} %constant.20.clone.refs_0_, bf16[48,288]{1,0:T(8,128)(2,1)} %constant.21.clone.refs_1_, bf16[96,144]{1,0:T(8,128)(2,1)} %constant.22.clone.refs_2_, ...), custom_call_target="tpu_custom_call" | custom-call | tf_op jit(solution)/shard_map/pallas_call | solution.py:446
  71.5 2.1 %broadcast_multiply_fusion = f32[16,96,128]{2,1,0:T(8,128)} fusion(f32[16,96,128]{2,1,0:T(8,128)} %shard_map.109), kind=kLoop, calls=%fused_computation | loop fusion | flops 196608 | bytes 1572864 | tf_op jit(solution)/shard_map/mul | solution.py:478

commit v6 on v5

--- a/solution.py
+++ b/solution.py
@@ -211,79 +211,74 @@
     loads[first_load].wait()
     own_load.wait()
 
-    def to_planes(i, carry):
-        pair = jnp.concatenate([given[2 * i], given[2 * i + 1]], axis=1)
+    pl.semaphore_wait(barrier, 2 * OWNERS + 3 - 2 * jnp.where(home, 1, 0))
+
+    def either(same, device, source, target, out_sem, in_sem):
+        here = jnp.logical_and(home, same)
+
+        @pl.when(here)
+        def _():
+            pltpu.make_async_copy(source, target, in_sem).start()
+
+        @pl.when(jnp.logical_not(here))
+        def _():
+            pltpu.make_async_remote_copy(
+                source, target, out_sem, in_sem, device_id=device, device_id_type=MESH
+            ).start()
+
+    def label_copy(i):
+        batch = (i + OWNERS - stick) % OWNERS // 4
+        either(i == member, own_computer(i), labels, columns.at[stick], label_send.at[0], label_recv.at[batch])
+
+    def plane_copy(z, i):
+        batch = (i + OWNERS - stick) % OWNERS // 4
+        source, target = sent.at[i, pl.ds(pl.multiple_of(32 * z, 32), 32)], blocks.at[z, stick]
+        either(i == member, own_computer(i), source, target, in_send.at[0], in_recv.at[z, batch])
+
+    def to_planes(step, carry):
+        bands = [(stick + 2 * step + i) % OWNERS for i in range(2)]
+        pair = jnp.concatenate([given[i] for i in bands], axis=1)
         pair = left_product(t["z_in"][...], pair)
-        sent[2 * i] = pair[:, :CAP]
-        sent[2 * i + 1] = pair[:, CAP:]
+        for i, band_index in enumerate(bands):
+            sent[band_index] = pair[:, CAP * i : CAP * (i + 1)]
+            label_copy(band_index)
+            plane_copy(0, band_index)
+        return carry
+
+    def send_planes(index, carry):
+        plane_copy(index // OWNERS, (stick + index) % OWNERS)
         return carry
 
     lax.fori_loop(0, OWNERS // 2, to_planes, 0)
-    pl.semaphore_wait(barrier, 2 * OWNERS + 3 - 2 * jnp.where(home, 1, 0))
-
-    def either(same, device, source, target, out_sem, in_sem, start):
-        here = jnp.logical_and(home, same)
-        if start:
-
-            @pl.when(here)
-            def _():
-                pltpu.make_async_copy(source, target, in_sem).start()
-
-        @pl.when(jnp.logical_not(here))
-        def _():
-            copy = pltpu.make_async_remote_copy(
-                source, target, out_sem, in_sem, device_id=device, device_id_type=MESH
-            )
-            if start:
-                copy.start()
-            else:
-                copy.wait_send()
-
-    def label_copy(i, start):
-        either(i == member, own_computer(i), labels, columns.at[stick], label_send.at[i], label_recv.at[stick], start)
-
-    def plane_copy(z, i, start):
-        source, target = sent.at[i, pl.ds(pl.multiple_of(32 * z, 32), 32)], blocks.at[z, stick]
-        either(i == member, own_computer(i), source, target, in_send.at[z, i], in_recv.at[z, stick], start)
-
-    def send_labels(step, carry):
-        label_copy((stick + step) % OWNERS, True)
-        return carry
-
-    def send_planes(index, carry):
-        plane_copy(index // OWNERS, (stick + index) % OWNERS, True)
-        return carry
-
-    lax.fori_loop(0, OWNERS, send_labels, 0)
-    lax.fori_loop(0, 3 * OWNERS, send_planes, 0)
+    lax.fori_loop(OWNERS, 3 * OWNERS, send_planes, 0)
 
     spans = lax.broadcasted_iota(jnp.int32, (128, CAP), 0) >> 4
 
     def arrive(ref, sem):
         pltpu.make_async_copy(ref, ref, sem).wait()
 
-    def field_copy(source, slot, z, index, device):
+    def field_copy(source, slot, z, device):
         return pltpu.make_async_remote_copy(
             fields.at[source, z],
             fields.at[slot, z],
-            field_send.at[index, z],
-            field_recv.at[slot, z],
+            field_send.at[0],
+            field_recv.at[slot - 1, z],
             device_id=device,
             device_id_type=MESH,
         )
 
     def outward(z):
         return [
-            field_copy(0, 2 + core, z, 0, to_upper),
-            field_copy(0, 2 + core, z, 1, to_lower),
-            field_copy(0, 1, z, 2, partner),
+            field_copy(0, 2 + core, z, to_upper),
+            field_copy(0, 2 + core, z, to_lower),
+            field_copy(0, 1, z, partner),
         ]
 
     def onward(z):
-        return field_copy(3 - core, 4, z, 3, partner)
+        return field_copy(3 - core, 4, z, partner)
 
     def pass_on(z):
-        arrive(fields.at[3 - core, z], field_recv.at[3 - core, z])
+        arrive(fields.at[3 - core, z], field_recv.at[2 - core, z])
         onward(z).start()
 
     def plane(z, carry):
@@ -294,12 +289,10 @@
 
             @pl.when(z == 0)
             def _():
-                for owner in owners:
-                    arrive(columns.at[owner], label_recv.at[owner])
+                arrive(columns.at[pl.ds(0, 4)], label_recv.at[step])
 
             hots, spreads = [], []
-            for owner in owners:
-                arrive(blocks.at[z, owner], in_recv.at[z, owner])
+            arrive(blocks.at[z, pl.ds(0, 4)], in_recv.at[z, step])
             for owner in owners:
                 row, span = slot_places(columns[owner])
                 keep = jnp.where(spans == span, 1.0, 0.0).astype(BF16)
@@ -353,9 +346,9 @@
         def _():
             pass_on(2)
 
-        arrive(fields.at[1, z], field_recv.at[1, z])
-        arrive(fields.at[2 + core, z], field_recv.at[2 + core, z])
-        arrive(fields.at[4, z], field_recv.at[4, z])
+        arrive(fields.at[1, z], field_recv.at[0, z])
+        arrive(fields.at[2 + core, z], field_recv.at[1 + core, z])
+        arrive(fields.at[4, z], field_recv.at[3, z])
         value = jnp.concatenate([fields[0, z] * fields[slot, z] for slot in range(1, 5)], axis=0)
         value = y_stage(x_stage(value, t["x"][...]), t["y_high"][...], t["y_low"][...])
         for i in range(4):
@@ -367,10 +360,10 @@
     value = value * jnp.concatenate([t["kernel"][...]] * 4, axis=0)
     work[...] = z_stage(value, t["z"][...]).reshape(4, 3, G, WIDE)
 
-    def result_copy(z, owner, start):
-        device = (owner, group)
+    def result_copy(z, owner):
+        batch = (member + OWNERS - owner) % OWNERS // 2
         source, target = found.at[z, owner], back.at[member, z]
-        either(owner == stick, device, source, target, out_send.at[z, owner], out_recv.at[member, z], start)
+        either(owner == stick, (owner, group), source, target, out_send.at[0], out_recv.at[batch])
 
     def backward(z, carry):
         value = jnp.concatenate([work[i, z] for i in range(4)], axis=0)
@@ -402,7 +395,7 @@
             result = jnp.concatenate(rows, axis=0)
             for i, owner in enumerate(owners):
                 found[z, owner] = result[:, CAP * i : CAP * (i + 1)]
-                result_copy(z, owner, True)
+                result_copy(z, owner)
             return carry
 
         lax.fori_loop(0, OWNERS // 2, pick, 0)
@@ -412,31 +405,30 @@
 
     def from_planes(step, carry):
         bands = [(stick + 2 * step + i) % OWNERS for i in range(2)]
-        for band_index in bands:
-            for z in range(3):
-                arrive(back.at[band_index, z], out_recv.at[band_index, z])
+        arrive(back.at[pl.ds(0, 2)], out_recv.at[step])
         pair = jnp.concatenate([back[band_index].reshape(2 * G, CAP) for band_index in bands], axis=1)
         pair = left_product(t["z_out"][...], pair)
         for i, band_index in enumerate(bands):
             ready[band_index] = pair[:, CAP * i : CAP * (i + 1)]
-            pltpu.make_async_copy(ready.at[band_index], out.at[band_index], out_store.at[band_index]).start()
+            pltpu.make_async_copy(ready.at[band_index], out.at[band_index], out_store.at[0]).start()
         return carry
 
     lax.fori_loop(0, OWNERS // 2, from_planes, 0)
-    for z in range(3):
-        for copy in outward(z):
-            copy.wait_send()
-        onward(z).wait_send()
-
-    def finish(i, carry):
-        label_copy(i, False)
-        for z in range(3):
-            plane_copy(z, i, False)
-            result_copy(z, i, False)
-        pltpu.make_async_copy(ready.at[i], out.at[i], out_store.at[i]).wait()
-        return carry
-
-    lax.fori_loop(0, OWNERS, finish, 0)
+    arrive(fields.at[pl.ds(0, 4)], field_send.at[0])
+
+    @pl.when(home)
+    def _():
+        arrive(sent.at[pl.ds(0, OWNERS - 1)], in_send.at[0])
+        arrive(columns.at[pl.ds(0, OWNERS - 1)], label_send.at[0])
+        arrive(found.at[:, pl.ds(0, OWNERS - 1)], out_send.at[0])
+
+    @pl.when(jnp.logical_not(home))
+    def _():
+        arrive(sent, in_send.at[0])
+        arrive(columns, label_send.at[0])
+        arrive(found, out_send.at[0])
+
+    pltpu.make_async_copy(ready, out, out_store.at[0]).wait()
 
 
 def on_device(sticks, stick_columns):
@@ -463,15 +455,15 @@
             pltpu.VMEM((OWNERS, 3, 32, CAP), F32),
             pltpu.VMEM((OWNERS, 2 * G, CAP), F32),
             dma((len(tables) + 1,)),
-            dma((3, OWNERS)),
-            dma((3, OWNERS)),
-            dma((OWNERS,)),
-            dma((OWNERS,)),
+            dma((1,)),
+            dma((3, 4)),
+            dma((1,)),
+            dma((4,)),
+            dma((1,)),
             dma((4, 3)),
-            dma((5, 3)),
-            dma((3, OWNERS)),
-            dma((OWNERS, 3)),
-            dma((OWNERS,)),
+            dma((1,)),
+            dma((OWNERS // 2,)),
+            dma((1,)),
         ],
         compiler_params=pltpu.CompilerParams(collective_id=0, has_side_effects=True, vmem_limit_bytes=56 << 20),
     )(sticks, stick_columns.reshape(1, CAP), *tables)

time: 74.3 us -> 72.1 us (0.970)
  Pallas kernels: 71.5 us -> 69.6 us
    pallas_call x1, Pallas kernels: 71.5 us -> 69.6 us  [on_device(): pl.pallas_call(exchange_kernel, out_shape=jax.ShapeDtypeStruct((OWNERS, 2...]
where the time goes in v6:
time: 72.1 us; the launch traced here: 71.7 us
  Pallas kernels  69.6 us (97%)
  other arithmetic  2.08 us (3%)
    pallas_call x1, Pallas kernels, on_device(): pl.pallas_call(exchange_kernel, out_shape=jax.ShapeDtypeStruct((OWNERS, 2...  69.6 us
    mul x1, other arithmetic, on_device(): return result * np.float32(G ** (-1.5))  2.08 us

profile of v6, /device:TPU:5, one launch (start us, length us, event | category | flops | bytes accessed | tf_op | source)
XLA Modules:
  0.0 71.7 jit_solution(7679989526784226439)
XLA Ops:
  0.0 69.6 %shard_map.109 = f32[16,96,128]{2,1,0:T(8,128)} custom-call(f32[16,96,128]{2,1,0:T(8,128)} %sticks.1, s32[1,128]{1,0:T(1,128)} %bitcast.1, bf16[48,144]{1,0:T(8,128)(2,1)} %constant.20.clone.refs_0_, bf16[48,288]{1,0:T(8,128)(2,1)} %constant.21.clone.refs_1_, bf16[96,144]{1,0:T(8,128)(2,1)} %constant.22.clone.refs_2_, ...), custom_call_target="tpu_custom_call" | custom-call | tf_op jit(solution)/shard_map/pallas_call | solution.py:438
  69.6 2.1 %broadcast_multiply_fusion = f32[16,96,128]{2,1,0:T(8,128)} fusion(f32[16,96,128]{2,1,0:T(8,128)} %shard_map.109), kind=kLoop, calls=%fused_computation | loop fusion | flops 196608 | bytes 1572864 | tf_op jit(solution)/shard_map/mul | solution.py:470

commit v7 on v6

--- a/solution.py
+++ b/solution.py
@@ -465,8 +465,8 @@
             dma((OWNERS // 2,)),
             dma((1,)),
         ],
-        compiler_params=pltpu.CompilerParams(collective_id=0, has_side_effects=True, vmem_limit_bytes=56 << 20),
-    )(sticks, stick_columns.reshape(1, CAP), *tables)
+        compiler_params=pltpu.CompilerParams(collective_id=0, has_side_effects=True, vmem_limit_bytes=48 << 20),
+    )(*[pltpu.with_memory_space_constraint(a, pltpu.HBM) for a in (sticks, stick_columns.reshape(1, CAP), *tables)])
     return result * np.float32(G**-1.5)
 
 

time: 72.1 us -> 71.2 us (0.988)
  other arithmetic: 2.08 us -> 0.95 us
    mul x1, other arithmetic: 2.08 us -> 0.95 us  [on_device(): return result * np.float32(G ** (-1.5))]
where the time goes in v7:
time: 71.2 us; the launch traced here: 70.5 us
  Pallas kernels  69.5 us (98%)
  other arithmetic  0.95 us (1%)
    pallas_call x1, Pallas kernels, on_device(): pl.pallas_call(exchange_kernel, out_shape=jax.ShapeDtypeStruct((OWNERS, 2...  69.5 us

profile of v7, /device:TPU:5, one launch (start us, length us, event | category | flops | bytes accessed | tf_op | source)
XLA Modules:
  0.0 70.5 jit_solution(8154979391854206947)
XLA Ops:
  0.0 69.5 %shard_map.109 = f32[16,96,128]{2,1,0:T(8,128)S(1)} custom-call(f32[16,96,128]{2,1,0:T(8,128)} %sticks.1, s32[1,128]{1,0:T(1,128)} %bitcast.1, bf16[48,144]{1,0:T(8,128)(2,1)} %constant.20.clone.refs_0_, bf16[48,288]{1,0:T(8,128)(2,1)} %constant.21.clone.refs_1_, bf16[96,144]{1,0:T(8,128)(2,1)} %constant.22.clone.refs_2_, ...), custom_call_target="tpu_custom_call" | custom-call | tf_op jit(solution)/shard_map/pallas_call | solution.py:438
  69.5 1.0 %broadcast_multiply_fusion = f32[16,96,128]{2,1,0:T(8,128)} fusion(f32[16,96,128]{2,1,0:T(8,128)S(1)} %shard_map.109), kind=kLoop, calls=%fused_computation | loop fusion | flops 196608 | bytes 1572864 | tf_op jit(solution)/shard_map/mul | solution.py:470

commit v8 on v7

--- a/solution.py
+++ b/solution.py
@@ -179,6 +179,7 @@
     partner = computer_of(pair, 1 - core, member)
     beyond = core * upper + (1 - core) * lower
     from_first, from_second = computer_of(beyond, 0, member), computer_of(beyond, 1, member)
+    to_same, from_same = computer_of(beyond, core, member), computer_of((2 * pair + 8 - beyond) % 8, core, member)
 
     barrier = pltpu.get_barrier_semaphore()
 
@@ -197,7 +198,7 @@
         return carry
 
     lax.fori_loop(0, OWNERS, greet, 0)
-    for device in (from_first, from_second, partner):
+    for device in (from_first, from_second, from_same, partner):
         signal(device)
 
     own_load = pltpu.make_async_copy(sticks, given, table_sem.at[count])
@@ -211,7 +212,7 @@
     loads[first_load].wait()
     own_load.wait()
 
-    pl.semaphore_wait(barrier, 2 * OWNERS + 3 - 2 * jnp.where(home, 1, 0))
+    pl.semaphore_wait(barrier, 2 * OWNERS + 4 - 2 * jnp.where(home, 1, 0))
 
     def either(same, device, source, target, out_sem, in_sem):
         here = jnp.logical_and(home, same)
@@ -329,22 +330,27 @@
         for copy in outward(z):
             copy.start()
 
+        @pl.when(z == 2)
+        def _():
+            field_copy(0, 4, z, to_same).start()
+
         return carry
 
     lax.fori_loop(0, 3, plane, 0)
-    pass_on(1)
-
     own = fields[0].reshape(ROWS, WIDE)
     value = x_stage(own * own, t["x"][...])
     value = y_stage(value, t["y_high"][...], t["y_low"][...])
     value = z_stage(value, t["z"][...]) * t["kernel"][...]
+    work[0] = value.reshape(3, G, WIDE)
+    pass_on(1)
+    value = work[0].reshape(ROWS, WIDE)
     value = y_stage(z_stage(value, t["z"][...]), t["y_high"][...], t["y_low"][...])
     total[...] = (x_stage(value, t["x"][...]) * own).reshape(3, G, WIDE)
 
     def forward(z, carry):
-        @pl.when(z == 1)
-        def _():
-            pass_on(2)
+        @pl.when(z == 2)
+        def _():
+            arrive(fields.at[3 - core, z], field_recv.at[2 - core, z])
 
         arrive(fields.at[1, z], field_recv.at[0, z])
         arrive(fields.at[2 + core, z], field_recv.at[1 + core, z])

time: 71.2 us -> 70.3 us (0.987)
  no operation moved by 1% of the time
where the time goes in v8:
time: 70.3 us
  Pallas kernels  69.3 us (99%)
  other arithmetic  0.95 us (1%)
    pallas_call x1, Pallas kernels, on_device(): pl.pallas_call(exchange_kernel, out_shape=jax.ShapeDtypeStruct((OWNERS, 2...  69.3 us

profile of v8, /device:TPU:5, one launch (start us, length us, event | category | flops | bytes accessed | tf_op | source)
XLA Modules:
  0.0 70.3 jit_solution(13276203320274374304)
XLA Ops:
  0.0 69.3 %shard_map.109 = f32[16,96,128]{2,1,0:T(8,128)S(1)} custom-call(f32[16,96,128]{2,1,0:T(8,128)} %sticks.1, s32[1,128]{1,0:T(1,128)} %bitcast.1, bf16[48,144]{1,0:T(8,128)(2,1)} %constant.20.clone.refs_0_, bf16[48,288]{1,0:T(8,128)(2,1)} %constant.21.clone.refs_1_, bf16[96,144]{1,0:T(8,128)(2,1)} %constant.22.clone.refs_2_, ...), custom_call_target="tpu_custom_call" | custom-call | tf_op jit(solution)/shard_map/pallas_call | solution.py:444
  69.3 1.0 %broadcast_multiply_fusion = f32[16,96,128]{2,1,0:T(8,128)} fusion(f32[16,96,128]{2,1,0:T(8,128)S(1)} %shard_map.109), kind=kLoop, calls=%fused_computation | loop fusion | flops 196608 | bytes 1572864 | tf_op jit(solution)/shard_map/mul | solution.py:476

commit v9 on v8

--- a/solution.py
+++ b/solution.py
@@ -317,10 +317,6 @@
                 if i != first_load:
                     load.wait()
 
-        @pl.when(z == 2)
-        def _():
-            pass_on(0)
-
         real = [grid[G * y : G * (y + 1), :128] for y in range(6)]
         imag = [grid[G * y : G * (y + 1), 128:] for y in range(6)]
         first = jnp.concatenate([a - b for a, b in zip(reflected(real), imag)], axis=1)
@@ -337,6 +333,7 @@
         return carry
 
     lax.fori_loop(0, 3, plane, 0)
+    pass_on(0)
     own = fields[0].reshape(ROWS, WIDE)
     value = x_stage(own * own, t["x"][...])
     value = y_stage(value, t["y_high"][...], t["y_low"][...])

time: 70.3 us -> 69.6 us (0.990)
  Pallas kernels: 69.3 us -> 68.2 us
    pallas_call x1, Pallas kernels: 69.3 us -> 68.2 us  [on_device(): pl.pallas_call(exchange_kernel, out_shape=jax.ShapeDtypeStruct((OWNERS, 2...]
where the time goes in v9:
time: 69.6 us; the launch traced here: 69.2 us
  Pallas kernels  68.2 us (98%)
  other arithmetic  0.95 us (1%)
    pallas_call x1, Pallas kernels, on_device(): pl.pallas_call(exchange_kernel, out_shape=jax.ShapeDtypeStruct((OWNERS, 2...  68.2 us

profile of v9, /device:TPU:5, one launch (start us, length us, event | category | flops | bytes accessed | tf_op | source)
XLA Modules:
  0.0 69.2 jit_solution(12579575006885406459)
XLA Ops:
  0.0 68.2 %shard_map.109 = f32[16,96,128]{2,1,0:T(8,128)S(1)} custom-call(f32[16,96,128]{2,1,0:T(8,128)} %sticks.1, s32[1,128]{1,0:T(1,128)} %bitcast.1, bf16[48,144]{1,0:T(8,128)(2,1)} %constant.20.clone.refs_0_, bf16[48,288]{1,0:T(8,128)(2,1)} %constant.21.clone.refs_1_, bf16[96,144]{1,0:T(8,128)(2,1)} %constant.22.clone.refs_2_, ...), custom_call_target="tpu_custom_call" | custom-call | tf_op jit(solution)/shard_map/pallas_call | solution.py:441
  68.2 1.0 %broadcast_multiply_fusion = f32[16,96,128]{2,1,0:T(8,128)} fusion(f32[16,96,128]{2,1,0:T(8,128)S(1)} %shard_map.109), kind=kLoop, calls=%fused_computation | loop fusion | flops 196608 | bytes 1572864 | tf_op jit(solution)/shard_map/mul | solution.py:473
